TPU v7x, 32 devices: a whole 2x2x4 slice. The times are simulated.
32 devices in a mesh: gx: 4 (over z), gy: 8 (over y, x, core).
Axes of the slice: x: 2, y: 2, z: 4, core: 2. Of those that a mesh axis runs over, the one named last changes fastest.
Arguments:
- grid_state: bfloat16 [8192, 1024], P(('gx', 'gy')), may hold values from -6 to 6
- mesh_state: bfloat16 [8192, 1024], P(('gx', 'gy')), may hold values from -6 to 6
- encode_block: int32 [8192], P(('gx', 'gy')), may hold values from 0 to 63, as said below
- neighbour_block: int32 [64], P(('gx', 'gy')), may hold values from 0 to 63, as said below
- decode_block: int32 [8192], P(('gx', 'gy')), may hold values from 0 to 63, as said below
- encode_grid_gain: float32 [1024], replicated, may hold values from 0.25 to 1.75
- encode_mesh_gain: float32 [1024], replicated, may hold values from 0.25 to 1.75
- process_gain: float32 [1024], replicated, may hold values from 0.25 to 1.75
- decode_grid_gain: float32 [1024], replicated, may hold values from 0.25 to 1.75
- decode_mesh_gain: float32 [1024], replicated, may hold values from 0.25 to 1.75
- encode_query: bfloat16 [1024, 1024], replicated, may hold values from -0.1875 to 0.1875
- encode_keyval: bfloat16 [1024, 2048], replicated, may hold values from -0.1875 to 0.1875
- encode_out: bfloat16 [1024, 1024], replicated, may hold values from -0.1875 to 0.1875
- process_qkv: bfloat16 [1024, 3072], replicated, may hold values from -0.1875 to 0.1875
- process_out: bfloat16 [1024, 1024], replicated, may hold values from -0.1875 to 0.1875
- decode_query: bfloat16 [1024, 1024], replicated, may hold values from -0.1875 to 0.1875
- decode_keyval: bfloat16 [1024, 2048], replicated, may hold values from -0.1875 to 0.1875
- decode_out: bfloat16 [1024, 1024], replicated, may hold values from -0.1875 to 0.1875
Outputs:
- grid_update: bfloat16 [8192, 1024], P(('gx', 'gy'))
Inputs may be any that keep to these rules, and one draw needn't show every extreme that they name: `encode_block`: block b lies on the b // 2-th device of the order of mesh nodes. The grid points of one device name the blocks of one device at most 16 times in all; every block is named by some grid point; in every draw some device's blocks are named exactly 16 times by the grid points of every device. `neighbour_block`: never b itself, and at most two blocks away from b. `decode_block`: block b lies on the b // 2-th device. The grid points of one device name the blocks of one device at most 16 times in all; every block is named; in every draw some device's blocks are named exactly 16 times by the grid points of every device.
All inputs are finite; a program needn't handle non-finite values.
Results may differ from a plain program's by a relative error of at most 0.015.
Values may be sent and summed in bfloat16 or wider, within the bound.
No kernel may reach another device: no remote copies, remote signals or barrier semaphores. Data moves between devices by JAX's collectives and lax.ppermute only.
A program may use at most 128 MiB of HBM per device.

v0:
```python
import functools

import jax
import jax.numpy as jnp
from jax import lax
from jax.experimental import pallas as pl
from jax.experimental.pallas import tpu as pltpu
from jax.sharding import PartitionSpec as P

HEADS = 16
BLOCK = 128
TILE = 512
LANES = 128
MASKED = -1e30
AXES = ("gx", "gy")
F32 = jnp.float32
BF16 = jnp.bfloat16
MIB = 1024 * 1024


def iota(shape, dim):
    return lax.broadcasted_iota(jnp.int32, shape, dim)


def floor_div(values, by):
    return jnp.floor((values.astype(F32) + 0.5) * (1.0 / by)).astype(jnp.int32)


def dot(left, right):
    return jnp.dot(left, right, preferred_element_type=F32)


def dot_t(left, right):
    return lax.dot_general(left, right, (((1,), (1,)), ((), ())), preferred_element_type=F32)


def dot_tl(left, right):
    return lax.dot_general(left, right, (((0,), (0,)), ((), ())), preferred_element_type=F32)


def normed(values, gain):
    wide = values.astype(F32)
    return wide * lax.rsqrt(jnp.mean(wide * wide, axis=-1, keepdims=True) + 1e-06) * gain


def block_hits(blocks, total_blocks):
    hits = iota((total_blocks, blocks.shape[1]), 0) == blocks
    return jnp.where(hits, 1.0, 0.0).astype(F32)


def slots_of(hits, per_device, capacity):
    total_blocks, points = hits.shape
    earlier = jnp.where(iota((points, points), 0) < iota((points, points), 1), 1.0, 0.0)
    before = dot(hits.astype(BF16), earlier.astype(BF16))
    counts = jnp.broadcast_to(jnp.sum(hits, axis=1, keepdims=True), (total_blocks, LANES))
    row, column = iota((total_blocks, total_blocks), 0), iota((total_blocks, total_blocks), 1)
    mates = (floor_div(row, per_device) == floor_div(column, per_device)) & (column < row)
    offset = dot(jnp.where(mates, 1.0, 0.0).astype(BF16), counts.astype(BF16))[:, :1]
    owner = floor_div(iota((total_blocks, 1), 0), per_device)
    base = owner.astype(F32) * capacity + offset
    return jnp.sum(hits * (base + before), axis=0, keepdims=True).astype(jnp.int32)


def placement(slot, slots):
    return jnp.where(iota((slots, slot.shape[1]), 0) == slot, 1.0, 0.0).astype(BF16)


def fill_kernel(per_device, capacity, me_ref, state_ref, encode_ref, decode_ref, gain_ref, packed_ref, counts_ref):
    devices, wide = counts_ref.shape
    total_blocks = wide // 2
    encode_hits = block_hits(encode_ref[...], total_blocks)
    slot = slots_of(encode_hits, per_device, capacity)
    place = placement(slot, devices * capacity)
    norm = normed(state_ref[...], gain_ref[...]).astype(BF16)
    packed_ref[...] = dot(place, norm).astype(BF16)
    decode_hits = block_hits(decode_ref[...], total_blocks)
    both = jnp.concatenate([encode_hits, decode_hits], axis=0).astype(BF16)
    counts = dot_t(jnp.ones((8, both.shape[1]), BF16), both)[:1]
    counts_ref[...] = jnp.where(iota((devices, wide), 0) == me_ref[0], counts, 0.0)


def start_weights(weight, held, ready, base, count, first=0):
    @pl.loop(0, count)
    def _(i):
        columns = pl.ds(pl.multiple_of(first + i * TILE, TILE), TILE)
        pltpu.make_async_copy(weight.at[:, columns], held.at[base + i], ready.at[base + i]).start()


def with_weights(rows, weight, held, ready, base, count, put):
    @pl.loop(0, count)
    def _(i):
        pltpu.make_async_copy(
            weight.at[:, pl.ds(0, TILE)], held.at[base + i], ready.at[base + i]
        ).wait()
        put(pl.ds(pl.multiple_of(i * TILE, TILE), TILE), dot(rows[...], held[base + i]))


def store_in(ref):
    def put(columns, values):
        ref[:, columns] = values.astype(ref.dtype)

    return put


def query_kernel(
    per_device, capacity, total_blocks, scale,
    mesh_ref, mesh_gain, encode_query, grid_ref, grid_gain, decode_query, decode_ref,
    query_ref, packed_ref,
    norm_ref, held, ready,
):
    count = encode_query.shape[1] // TILE
    start_weights(decode_query, held, ready, 0, count)
    start_weights(encode_query, held, ready, count, count)
    norm_ref[...] = normed(grid_ref[...], grid_gain[...]).astype(BF16)
    slots = packed_ref.shape[0]
    slot = slots_of(block_hits(decode_ref[...], total_blocks), per_device, capacity)
    place = placement(slot, slots)

    def put_packed(columns, values):
        rounded = (values.astype(BF16).astype(F32) * scale).astype(BF16)
        packed_ref[:, columns] = dot(place, rounded).astype(BF16)

    with_weights(norm_ref, decode_query, held, ready, 0, count, put_packed)
    norm_ref[...] = normed(mesh_ref[...], mesh_gain[...]).astype(BF16)

    def put_query(columns, values):
        query_ref[:, columns] = (values.astype(BF16).astype(F32) * scale).astype(BF16)

    with_weights(norm_ref, encode_query, held, ready, count, count, put_query)


def own_counts(counts, me, per_device, first):
    wide = counts.shape[1]
    wanted = iota((8, wide), 1) == (iota((8, wide), 0) + (first + me * per_device))
    wanted = wanted & (iota((8, wide), 0) < per_device)
    return dot_t(jnp.where(wanted, 1.0, 0.0).astype(BF16), counts.astype(BF16)).astype(BF16)


def even_lanes(shape, head_size):
    return iota(shape, len(shape) - 1) < head_size


def split_heads(values, head_size):
    even = even_lanes(values.shape, head_size)
    zero = jnp.zeros_like(values)
    return jnp.concatenate([jnp.where(even, values, zero), jnp.where(even, zero, values)], axis=0)


def join_heads(values, head_size):
    rows = values.shape[0] // 2
    even = even_lanes((rows, values.shape[1]), head_size)
    return jnp.where(even, values[:rows], values[rows:])


def encode_kernel(
    per_device, capacity, head_size,
    me_ref, received_ref, counts_ref, query_ref, mesh_ref, gain_ref, keyval_w, out_w,
    mid_ref, norm_ref,
    keyval, attended, bias, held, ready,
):
    features = query_ref.shape[1]
    slots = received_ref.shape[0]
    devices = counts_ref.shape[0]
    kv_count, out_count = keyval_w.shape[1] // TILE, features // TILE
    start_weights(keyval_w, held, ready, 0, kv_count)
    start_weights(out_w, held, ready, kv_count, out_count)
    with_weights(received_ref, keyval_w, held, ready, 0, kv_count, store_in(keyval))

    mine = own_counts(counts_ref[...], me_ref[0], per_device, 0)
    sender = floor_div(iota((devices, slots), 1), capacity) == iota((devices, slots), 0)
    filled = dot(mine, jnp.where(sender, 1.0, 0.0).astype(BF16))
    lane = iota((1, slots), 1)
    place = (lane - floor_div(lane, capacity) * capacity).astype(F32)
    begin = jnp.zeros((1, slots), F32)
    for block in range(per_device):
        end = begin + filled[block : block + 1]
        bias[block : block + 1] = jnp.where((place >= begin) & (place < end), 0.0, MASKED)
        begin = end

    @pl.loop(0, features // LANES)
    def _(pair):
        columns = pl.ds(pl.multiple_of(pair * LANES, LANES), LANES)
        value_columns = pl.ds(pl.multiple_of(features + pair * LANES, LANES), LANES)
        keys, values = keyval[:, columns], keyval[:, value_columns]
        for block in range(per_device):
            rows = pl.ds(block * BLOCK, BLOCK)
            queries = split_heads(query_ref[rows, columns], head_size)
            scores = dot_t(queries, keys) + bias[block : block + 1]
            powers = jnp.exp(scores - jnp.max(scores, axis=-1, keepdims=True))
            sums = jnp.sum(powers, axis=-1, keepdims=True)
            output = dot(powers.astype(BF16), values) / sums
            attended[rows, columns] = join_heads(output, head_size).astype(BF16)

    def put_mid(columns, values):
        mid_ref[:, columns] = (mesh_ref[:, columns].astype(F32) + values).astype(BF16)

    with_weights(attended, out_w, held, ready, kv_count, out_count, put_mid)
    norm_ref[...] = normed(mid_ref[...], gain_ref[...]).astype(BF16)


def process_kernel(
    per_device, capacity, head_size, scale,
    me_ref, position_ref, counts_ref, qkv_ref, before_ref, norm_ref, after_ref, mid_ref, queries_ref, gain_ref,
    qkv_w, out_w, decode_w,
    answers_ref,
    chosen, other, attended, mesh_out, held, ready,
):
    features = mid_ref.shape[1]
    slots, devices = queries_ref.shape[0], counts_ref.shape[0]
    kv_count, out_count = 2 * features // TILE, features // TILE
    start_weights(qkv_w, held, ready, 0, kv_count, features)
    start_weights(out_w, held, ready, kv_count, out_count)
    start_weights(decode_w, held, ready, kv_count + out_count, kv_count)
    for block in range(per_device):
        rows = pl.ds(block * BLOCK, BLOCK)
        position = position_ref[block]
        for side, source in enumerate((before_ref, norm_ref, after_ref)):
            for place in range(per_device):
                @pl.when(position == side * per_device + place)
                def _():
                    chosen[rows] = source[pl.ds(place * BLOCK, BLOCK)]

    with_weights(chosen, qkv_w, held, ready, 0, kv_count, store_in(other))

    @pl.loop(0, features // LANES)
    def _(pair):
        columns = pl.ds(pl.multiple_of(pair * LANES, LANES), LANES)
        second = pl.ds(pl.multiple_of(features + pair * LANES, LANES), LANES)
        third = pl.ds(pl.multiple_of(2 * features + pair * LANES, LANES), LANES)
        for block in range(per_device):
            rows = pl.ds(block * BLOCK, BLOCK)
            queries = split_heads((qkv_ref[rows, columns].astype(F32) * scale).astype(BF16), head_size)
            keys = jnp.concatenate([qkv_ref[rows, second], other[rows, columns]], axis=0)
            values = jnp.concatenate([qkv_ref[rows, third], other[rows, second]], axis=0)
            scores = dot_t(queries, keys)
            powers = jnp.exp(scores - jnp.max(scores, axis=-1, keepdims=True))
            sums = jnp.sum(powers, axis=-1, keepdims=True)
            output = dot(powers.astype(BF16), values) / sums
            attended[rows, columns] = join_heads(output, head_size).astype(BF16)

    def put_out(columns, values):
        mesh_out[:, columns] = (mid_ref[:, columns].astype(F32) + values).astype(BF16)

    with_weights(attended, out_w, held, ready, kv_count, out_count, put_out)
    chosen[...] = normed(mesh_out[...], gain_ref[...]).astype(BF16)
    with_weights(chosen, decode_w, held, ready, kv_count + out_count, kv_count, store_in(other))

    total_blocks = counts_ref.shape[1] // 2
    mine = own_counts(counts_ref[...], me_ref[0], per_device, total_blocks)
    sender = floor_div(iota((slots, devices), 0), capacity) == iota((slots, devices), 1)
    filled = dot_t(jnp.where(sender, 1.0, 0.0).astype(BF16), mine)
    row = iota((slots, 1), 0)
    place = (row - floor_div(row, capacity) * capacity).astype(F32)
    reads, begin = [], jnp.zeros((slots, 1), F32)
    for block in range(per_device):
        end = begin + filled[:, block : block + 1]
        reads.append(jnp.broadcast_to(jnp.where((place >= begin) & (place < end), 1.0, 0.0), (slots, BLOCK)))
        begin = end

    @pl.loop(0, features // LANES)
    def _(pair):
        columns = pl.ds(pl.multiple_of(pair * LANES, LANES), LANES)
        second = pl.ds(pl.multiple_of(features + pair * LANES, LANES), LANES)
        queries = queries_ref[:, columns]
        even = even_lanes((slots, LANES), head_size)
        outputs = []
        for head in range(LANES // head_size):
            picked = jnp.where(even if head == 0 else ~even, queries, jnp.zeros_like(queries))
            scores = dot_t(picked, other[:, columns])
            chosen_scores = scores[:, :BLOCK]
            for block in range(1, per_device):
                here = scores[:, block * BLOCK : (block + 1) * BLOCK]
                chosen_scores = jnp.where(reads[block] > 0.5, here, chosen_scores)
            powers = jnp.exp(chosen_scores - jnp.max(chosen_scores, axis=-1, keepdims=True))
            sums = jnp.sum(powers, axis=-1, keepdims=True)
            spread = jnp.concatenate(
                [jnp.where(reads[block] > 0.5, powers, 0.0).astype(BF16) for block in range(per_device)], axis=1
            )
            outputs.append(dot(spread, other[:, second]) / sums)
        answers_ref[:, columns] = jnp.where(even, outputs[0], outputs[1]).astype(BF16)


def unpack_kernel(
    per_device, capacity, total_blocks, replies_ref, decode_ref, out_w, update_ref, decoded, held, ready
):
    count = out_w.shape[1] // TILE
    start_weights(out_w, held, ready, 0, count)
    slot = slots_of(block_hits(decode_ref[...], total_blocks), per_device, capacity)
    place = placement(slot, replies_ref.shape[0])
    decoded[...] = dot_tl(place, replies_ref[...]).astype(BF16)
    with_weights(decoded, out_w, held, ready, 0, count, store_in(update_ref))


VMEM, SMEM, ANY = pltpu.VMEM, pltpu.SMEM, pl.ANY


def call(kernel, operands, outs, scratch, name, limit, flops=0):
    spaces = [space for space, _ in operands]
    return pl.pallas_call(
        kernel,
        out_shape=[jax.ShapeDtypeStruct(shape, kind) for shape, kind in outs],
        in_specs=[pl.BlockSpec(memory_space=space) for space in spaces],
        out_specs=[pl.BlockSpec(memory_space=VMEM) for _ in outs],
        scratch_shapes=scratch,
        name=name,
        cost_estimate=pl.CostEstimate(flops=flops, bytes_accessed=4 * MIB, transcendentals=0),
        compiler_params=pltpu.CompilerParams(vmem_limit_bytes=limit * MIB),
    )(*[value for _, value in operands])


def weights_held(count, features):
    return [VMEM((count, features, TILE), BF16), pltpu.SemaphoreType.DMA((count,))]


def on_device(
    grid_state,
    mesh_state,
    encode_block,
    neighbour_block,
    decode_block,
    encode_grid_gain,
    encode_mesh_gain,
    process_gain,
    decode_grid_gain,
    decode_mesh_gain,
    encode_query,
    encode_keyval,
    encode_out,
    process_qkv,
    process_out,
    decode_query,
    decode_keyval,
    decode_out,
):
    devices = lax.axis_size(AXES)
    me = lax.axis_index(AXES)
    grid_count, features = grid_state.shape
    mesh_rows = mesh_state.shape[0]
    per_device = mesh_rows // BLOCK
    total_blocks = per_device * devices
    capacity = max(4, 2 * grid_count // devices)
    slots = devices * capacity
    head_size = features // HEADS
    scale = head_size ** (-0.5)
    tiles = features // TILE
    me_row = me.astype(jnp.int32).reshape(1)
    position = neighbour_block - me * per_device + per_device
    encode_row, decode_row = encode_block.reshape(1, -1), decode_block.reshape(1, -1)
    gains = [
        gain.reshape(1, -1)
        for gain in (encode_grid_gain, encode_mesh_gain, process_gain, decode_grid_gain, decode_mesh_gain)
    ]

    def exchange(rows):
        return lax.all_to_all(
            rows.reshape(devices, capacity, features), AXES, split_axis=0, concat_axis=0, tiled=True
        ).reshape(slots, features)

    packed, counts = call(
        functools.partial(fill_kernel, per_device, capacity),
        [(SMEM, me_row), (VMEM, grid_state), (VMEM, encode_row), (VMEM, decode_row), (VMEM, gains[0])],
        [((slots, features), BF16), ((devices, 2 * total_blocks), F32)],
        [],
        "fill",
        32,
        flops=600_000_000,
    )
    received = exchange(packed)
    step = 1
    while step < devices:
        counts = counts + lax.ppermute(counts, AXES, [(i, i ^ step) for i in range(devices)])
        step *= 2
    query, packed_queries = call(
        functools.partial(query_kernel, per_device, capacity, total_blocks, scale),
        [
            (VMEM, mesh_state), (VMEM, gains[1]), (ANY, encode_query),
            (VMEM, grid_state), (VMEM, gains[3]), (ANY, decode_query), (VMEM, decode_row),
        ],
        [((mesh_rows, features), BF16), ((slots, features), BF16)],
        [VMEM((grid_count, features), BF16), *weights_held(2 * tiles, features)],
        "queries",
        32,
        flops=2_000_000_000,
    )
    arrived_queries = exchange(packed_queries)
    mesh_mid, process_norm = call(
        functools.partial(encode_kernel, per_device, capacity, head_size),
        [
            (SMEM, me_row), (VMEM, received), (VMEM, counts), (VMEM, query), (VMEM, mesh_state), (VMEM, gains[2]),
            (ANY, encode_keyval), (ANY, encode_out),
        ],
        [((mesh_rows, features), BF16), ((mesh_rows, features), BF16)],
        [
            VMEM((slots, 2 * features), BF16),
            VMEM((mesh_rows, features), BF16),
            VMEM((8, slots), F32),
            *weights_held(3 * tiles, features),
        ],
        "encode",
        32,
        flops=5_000_000_000,
    )
    before = lax.ppermute(process_norm, AXES, [(i, i + 1) for i in range(devices - 1)])
    after = lax.ppermute(process_norm, AXES, [(i + 1, i) for i in range(devices - 1)])
    mesh_qkv = dot(process_norm, process_qkv).astype(BF16)
    (answers,) = call(
        functools.partial(process_kernel, per_device, capacity, head_size, scale),
        [
            (SMEM, me_row), (SMEM, position), (VMEM, counts), (VMEM, mesh_qkv), (VMEM, before), (VMEM, process_norm),
            (VMEM, after), (VMEM, mesh_mid), (VMEM, arrived_queries), (VMEM, gains[4]),
            (ANY, process_qkv), (ANY, process_out), (ANY, decode_keyval),
        ],
        [((slots, features), BF16)],
        [
            VMEM((mesh_rows, features), BF16),
            VMEM((mesh_rows, 2 * features), BF16),
            VMEM((mesh_rows, features), BF16),
            VMEM((mesh_rows, features), BF16),
            *weights_held(5 * tiles, features),
        ],
        "process",
        40,
        flops=6_000_000_000,
    )
    replies = exchange(answers)
    (update,) = call(
        functools.partial(unpack_kernel, per_device, capacity, total_blocks),
        [(VMEM, replies), (VMEM, decode_row), (ANY, decode_out)],
        [((grid_count, features), BF16)],
        [VMEM((grid_count, features), BF16), *weights_held(tiles, features)],
        "unpack",
        32,
        flops=1_000_000_000,
    )
    return update


def solution(mesh):
    in_specs = (P(AXES, None), P(AXES, None), P(AXES), P(AXES), P(AXES), *[P()] * 13)
    return jax.shard_map(
        on_device, mesh=mesh, in_specs=in_specs, out_specs=P(AXES, None), check_vma=False
    )
```

profile of v0, /device:TPU:0, one launch (start us, length us, event | category | flops | bytes accessed | tf_op | source)
XLA Modules:
  0.0 158.3 jit_solution(16670342859607491623)
XLA Ops:
  0.0 1.1 copy-done.7
  1.1 0.7 copy-done.10
  1.8 0.7 copy-done.15
  2.5 0.7 copy-done.16
  3.1 1.7 %fill.1 = (bf16[512,1024]{1,0:T(8,128)(2,1)}, f32[32,128]{1,0:T(8,128)S(1)}) custom-call(s32[1]{0:T(128)} %bitcast.me_ref, bf16[256,1024]{1,0:T(8,128)(2,1)S(1)} %copy-done.7, s32[1,256]{1,0:T(1,128)S(1)} %bitcast.25, s32[1,256]{1,0:T(1,128)S(1)} %bitcast.26, f32[1,1024]{1,0:T(1,128)S(1)} %bitcast.20), custom_call_target="tpu_custom_call" | custom-call | flops 600000000 | bytes 4194304 | tf_op jit(solution)/shard_map/fill/pallas_call | solution.py:299
  4.9 7.3 %all-to-all-start = ((bf16[32,16,1024]{2,1,0:T(8,128)(2,1)}), bf16[32,16,1024]{2,1,0:T(8,128)(2,1)S(1)}, u32[]{:S(2)}, u32[]{:S(2)}) async-start(bf16[32,16,1024]{2,1,0:T(8,128)(2,1)} %bitcast.4), calls=%async_computation | async-start | bytes 2097152 | tf_op jit(solution)/shard_map/all_to_all | solution.py:355
  12.2 0.0 copy-done.17
  12.2 0.0 copy-done.12
  12.3 0.0 copy-start.2
  12.3 1.6 copy-done.2
  13.9 1.6 %copy-done.3 = bf16[1024,1024]{1,0:T(8,128)(2,1)S(1)} copy-done((bf16[1024,1024]{1,0:T(8,128)(2,1)S(1)}, bf16[1024,1024]{1,0:T(8,128)(2,1)}, u32[]{:S(2)}) %copy-start.3) | copy-done | bytes 2097176
  15.4 4.1 %queries.1 = (bf16[256,1024]{1,0:T(8,128)(2,1)S(1)}, bf16[512,1024]{1,0:T(8,128)(2,1)}) custom-call(bf16[256,1024]{1,0:T(8,128)(2,1)S(1)} %copy-done.9, f32[1,1024]{1,0:T(1,128)S(1)} %bitcast.21, bf16[1024,1024]{1,0:T(8,128)(2,1)S(1)} %copy-done.2, bf16[256,1024]{1,0:T(8,128)(2,1)S(1)} %copy-done.8, f32[1,1024]{1,0:T(1,128)S(1)} %bitcast.22, ...), custom_call_target="tpu_custom_call" | custom-call | flops 2000000000 | bytes 4194304 | tf_op jit(solution)/shard_map/queries/pallas_call | solution.py:299
  19.5 0.0 copy-start.18
  19.6 0.8 copy-done.18
  20.3 18.1 %all-to-all-done = bf16[32,16,1024]{2,1,0:T(8,128)(2,1)S(1)} async-done(((bf16[32,16,1024]{2,1,0:T(8,128)(2,1)}), bf16[32,16,1024]{2,1,0:T(8,128)(2,1)S(1)}, u32[]{:S(2)}, u32[]{:S(2)}) %all-to-all-start) | async-done | bytes 1048608 | tf_op jit(solution)/shard_map/all_to_all | solution.py:355
  38.4 3.6 %all-to-all-start.1 = ((bf16[32,16,1024]{2,1,0:T(8,128)(2,1)}), bf16[32,16,1024]{2,1,0:T(8,128)(2,1)S(1)}, u32[]{:S(2)}, u32[]{:S(2)}) async-start(bf16[32,16,1024]{2,1,0:T(8,128)(2,1)} %bitcast.9), calls=%async_computation.1 | async-start | bytes 2097152 | tf_op jit(solution)/shard_map/all_to_all | solution.py:355
  42.0 0.3 collective-permute-start
  42.4 0.9 collective-permute-done
  43.3 1.8 %collective-permute-start.1 = (f32[32,128]{1,0:T(8,128)S(1)}, f32[32,128]{1,0:T(8,128)S(1)}, u32[]{:S(2)}, u32[]{:S(2)}) collective-permute-start(f32[32,128]{1,0:T(8,128)S(1)} %add.23), channel_id=1, source_target_pairs={{0,2},{1,3},{2,0},{3,1},{4,6},{5,7},{6,4},{7,5},{8,10},{9,11},{10,... | collective-permute-start | bytes 49160 | tf_op jit(solution)/shard_map/ppermute | solution.py:371
  45.1 5.0 %collective-permute-done.1 = f32[32,128]{1,0:T(8,128)S(1)} collective-permute-done((f32[32,128]{1,0:T(8,128)S(1)}, f32[32,128]{1,0:T(8,128)S(1)}, u32[]{:S(2)}, u32[]{:S(2)}) %collective-permute-start.1) | collective-permute-done | bytes 16416 | tf_op jit(solution)/shard_map/ppermute | solution.py:371
  50.1 2.7 %collective-permute-start.2 = (f32[32,128]{1,0:T(8,128)S(1)}, f32[32,128]{1,0:T(8,128)S(1)}, u32[]{:S(2)}, u32[]{:S(2)}) collective-permute-start(f32[32,128]{1,0:T(8,128)S(1)} %add.24), channel_id=1, source_target_pairs={{0,4},{1,5},{2,6},{3,7},{4,0},{5,1},{6,2},{7,3},{8,12},{9,13},{10,... | collective-permute-start | bytes 49160 | tf_op jit(solution)/shard_map/ppermute | solution.py:371
  52.7 1.9 %collective-permute-done.2 = f32[32,128]{1,0:T(8,128)S(1)} collective-permute-done((f32[32,128]{1,0:T(8,128)S(1)}, f32[32,128]{1,0:T(8,128)S(1)}, u32[]{:S(2)}, u32[]{:S(2)}) %collective-permute-start.2) | collective-permute-done | bytes 16416 | tf_op jit(solution)/shard_map/ppermute | solution.py:371
  54.7 0.3 collective-permute-start.3
  55.0 5.0 %collective-permute-done.3 = f32[32,128]{1,0:T(8,128)S(1)} collective-permute-done((f32[32,128]{1,0:T(8,128)S(1)}, f32[32,128]{1,0:T(8,128)S(1)}, u32[]{:S(2)}, u32[]{:S(2)}) %collective-permute-start.3) | collective-permute-done | bytes 16416 | tf_op jit(solution)/shard_map/ppermute | solution.py:371
  60.0 4.5 %collective-permute-start.4 = (f32[32,128]{1,0:T(8,128)S(1)}, f32[32,128]{1,0:T(8,128)S(1)}, u32[]{:S(2)}, u32[]{:S(2)}) collective-permute-start(f32[32,128]{1,0:T(8,128)S(1)} %add.26), channel_id=1, source_target_pairs={{0,16},{1,17},{2,18},{3,19},{4,20},{5,21},{6,22},{7,23},{8,24},{9,... | collective-permute-start | bytes 49160 | tf_op jit(solution)/shard_map/ppermute | solution.py:371
  64.5 4.4 %collective-permute-done.4 = f32[32,128]{1,0:T(8,128)S(1)} collective-permute-done((f32[32,128]{1,0:T(8,128)S(1)}, f32[32,128]{1,0:T(8,128)S(1)}, u32[]{:S(2)}, u32[]{:S(2)}) %collective-permute-start.4) | collective-permute-done | bytes 16416 | tf_op jit(solution)/shard_map/ppermute | solution.py:371
  68.9 0.0 copy-done.13
  69.0 2.2 %copy-done = bf16[1024,2048]{1,0:T(8,128)(2,1)S(1)} copy-done((bf16[1024,2048]{1,0:T(8,128)(2,1)S(1)}, bf16[1024,2048]{1,0:T(8,128)(2,1)}, u32[]{:S(2)}) %copy-start) | copy-done | bytes 4194328
  71.1 1.6 %copy-done.4 = bf16[1024,1024]{1,0:T(8,128)(2,1)S(1)} copy-done((bf16[1024,1024]{1,0:T(8,128)(2,1)S(1)}, bf16[1024,1024]{1,0:T(8,128)(2,1)}, u32[]{:S(2)}) %copy-start.4) | copy-done | bytes 2097176
  72.7 1.0 copy-done.19
  73.8 11.4 %encode.1 = (bf16[256,1024]{1,0:T(8,128)(2,1)S(1)}, bf16[256,1024]{1,0:T(8,128)(2,1)S(1)}) custom-call(s32[1]{0:T(128)} %bitcast.me_ref, bf16[512,1024]{1,0:T(8,128)(2,1)S(1)} %bitcast.17, f32[32,128]{1,0:T(8,128)S(1)} %add.27.counts_ref, bf16[256,1024]{1,0:T(8,128)(2,1)S(1)} %copy-done.19, bf16[256,1024]{1,0:T(8,128)(2,1)S(1)} %copy-done.9, ...), custom_call_target="tpu_custom_call" | custom-call | flops 5000000000 | bytes 4194304 | tf_op jit(solution)/shard_map/encode/pallas_call | solution.py:299
  85.2 0.0 copy-start.21
  85.2 0.8 copy-done.21
  86.0 1.4 collective-permute-start.6
  87.4 3.1 %collective-permute-start.5 = (bf16[256,1024]{1,0:T(8,128)(2,1)S(1)}, bf16[256,1024]{1,0:T(8,128)(2,1)S(1)}, u32[]{:S(2)}, u32[]{:S(2)}) collective-permute-start(bf16[256,1024]{1,0:T(8,128)(2,1)S(1)} %get-tuple-element.14.norm_ref), channel_id=1, source_target_pairs={{0,1},{1,2},{2,3},{3,4},{4,5},{5,6},{6,7},{7,8},{8,9},{9,10},{10,1... | collective-permute-start | bytes 1572872 | tf_op jit(solution)/shard_map/ppermute | solution.py:403
  90.5 5.8 %convolution_convert_fusion.qkv_ref = bf16[256,3072]{1,0:T(8,128)(2,1)} fusion(bf16[256,1024]{1,0:T(8,128)(2,1)S(1)} %get-tuple-element.14.norm_ref, bf16[1024,3072]{1,0:T(8,128)(2,1)} %qkv_w.1), kind=kOutput, calls=%fused_computation | convolution fusion | flops 1611399168 | bytes 8388608 | tf_op jit(solution)/shard_map/dot_general | solution.py:30
  96.2 0.0 all-to-all-done.1
  96.2 0.0 collective-permute-done.6.after_ref
  96.3 0.0 collective-permute-done.5.before_ref
  96.3 0.0 copy-start.1
  96.3 2.2 %copy-done.1 = bf16[1024,2048]{1,0:T(8,128)(2,1)S(1)} copy-done((bf16[1024,2048]{1,0:T(8,128)(2,1)S(1)}, bf16[1024,2048]{1,0:T(8,128)(2,1)}, u32[]{:S(2)}) %copy-start.1) | copy-done | bytes 4194328
  98.5 1.6 %copy-done.5 = bf16[1024,1024]{1,0:T(8,128)(2,1)S(1)} copy-done((bf16[1024,1024]{1,0:T(8,128)(2,1)S(1)}, bf16[1024,1024]{1,0:T(8,128)(2,1)}, u32[]{:S(2)}) %copy-start.5) | copy-done | bytes 2097176
  100.1 1.4 copy-done.20
  101.5 1.0 copy-done.22
  102.5 17.8 %process.1 = bf16[512,1024]{1,0:T(8,128)(2,1)S(1)} custom-call(s32[1]{0:T(128)} %bitcast.me_ref, s32[2]{0:T(128)S(1)} %subtract_add_fusion.position_ref, f32[32,128]{1,0:T(8,128)S(1)} %add.27.counts_ref, bf16[256,3072]{1,0:T(8,128)(2,1)S(1)} %copy-done.20, bf16[256,1024]{1,0:T(8,128)(2,1)S(1)} %collective-permute-done.5.before_ref, ...), custom_call_target="tpu_custom_call" | custom-call | flops 6000000000 | bytes 4194304 | tf_op jit(solution)/shard_map/process/pallas_call | solution.py:299
  120.3 35.3 %all_to_all.15 = bf16[32,16,1024]{2,1,0:T(8,128)(2,1)S(1)} all-to-all(bf16[32,16,1024]{2,1,0:T(8,128)(2,1)S(1)} %bitcast.18), channel_id=1, replica_groups=mesh['gx'=4,'gy'=8] {'gx','gy'}, dimensions={0} | all-to-all | bytes 2097152 | tf_op jit(solution)/shard_map/all_to_all | solution.py:355
  155.6 0.0 copy-done.6
  155.6 2.8 %unpack.1 = bf16[256,1024]{1,0:T(8,128)(2,1)} custom-call(bf16[512,1024]{1,0:T(8,128)(2,1)S(1)} %bitcast.19, s32[1,256]{1,0:T(1,128)S(1)} %bitcast.28, bf16[1024,1024]{1,0:T(8,128)(2,1)S(1)} %copy-done.6), custom_call_target="tpu_custom_call" | custom-call | flops 1000000000 | bytes 4194304 | tf_op jit(solution)/shard_map/unpack/pallas_call | solution.py:299
  (31 shorter events, 0.1 us)
Async XLA Ops:
  0.0 12.2 %copy-start.17 = (s32[256]{0:T(256)S(1)}, s32[256]{0:T(256)}, u32[]{:S(2)}) copy-start(s32[256]{0:T(256)} %param.22) | copy-start | bytes 3076
  0.0 12.2 %copy-start.12 = (f32[1024]{0:T(1024)S(1)}, f32[1024]{0:T(1024)}, u32[]{:S(2)}) copy-start(f32[1024]{0:T(1024)} %param.26) | copy-start | bytes 12292
  0.0 12.2 %copy-start.11 = (f32[1024]{0:T(1024)S(1)}, f32[1024]{0:T(1024)}, u32[]{:S(2)}) copy-start(f32[1024]{0:T(1024)} %param.24) | copy-start | bytes 12292
  0.0 1.1 copy-start.7
  1.1 0.7 copy-start.10
  1.8 0.7 copy-start.15
  2.5 0.7 copy-start.16
  3.1 9.1 %copy-start.8 = (bf16[256,1024]{1,0:T(8,128)(2,1)S(1)}, bf16[256,1024]{1,0:T(8,128)(2,1)}, u32[]{:S(2)}) copy-start(bf16[256,1024]{1,0:T(8,128)(2,1)} %grid_ref.1) | copy-start | bytes 1572868
  3.1 9.1 %copy-start.9 = (bf16[256,1024]{1,0:T(8,128)(2,1)S(1)}, bf16[256,1024]{1,0:T(8,128)(2,1)}, u32[]{:S(2)}) copy-start(bf16[256,1024]{1,0:T(8,128)(2,1)} %mesh_ref.3) | copy-start | bytes 1572868
  4.9 33.5 %all-to-all-start = ((bf16[32,16,1024]{2,1,0:T(8,128)(2,1)}), bf16[32,16,1024]{2,1,0:T(8,128)(2,1)S(1)}, u32[]{:S(2)}, u32[]{:S(2)}) async-start(bf16[32,16,1024]{2,1,0:T(8,128)(2,1)} %bitcast.4), calls=%async_computation | async-start | bytes 2097152 | tf_op jit(solution)/shard_map/all_to_all | solution.py:355
  12.3 1.6 %copy-start.2 = (bf16[1024,1024]{1,0:T(8,128)(2,1)S(1)}, bf16[1024,1024]{1,0:T(8,128)(2,1)}, u32[]{:S(2)}) copy-start(bf16[1024,1024]{1,0:T(8,128)(2,1)} %encode_query.1) | copy-start | bytes 6291460
  13.8 1.6 %copy-start.3 = (bf16[1024,1024]{1,0:T(8,128)(2,1)S(1)}, bf16[1024,1024]{1,0:T(8,128)(2,1)}, u32[]{:S(2)}) copy-start(bf16[1024,1024]{1,0:T(8,128)(2,1)} %decode_query.1) | copy-start | bytes 6291460
  15.4 49.1 %copy-start.23 = (s32[2]{0:T(128)S(1)}, s32[2]{0:T(128)}, u32[]{:S(2)}) copy-start(s32[2]{0:T(128)} %param.21) | copy-start | bytes 28
  15.4 53.5 %copy-start.13 = (f32[1024]{0:T(1024)S(1)}, f32[1024]{0:T(1024)}, u32[]{:S(2)}) copy-start(f32[1024]{0:T(1024)} %param.25) | copy-start | bytes 12292
  19.5 0.8 copy-start.18
  38.4 57.8 %all-to-all-start.1 = ((bf16[32,16,1024]{2,1,0:T(8,128)(2,1)}), bf16[32,16,1024]{2,1,0:T(8,128)(2,1)S(1)}, u32[]{:S(2)}, u32[]{:S(2)}) async-start(bf16[32,16,1024]{2,1,0:T(8,128)(2,1)} %bitcast.9), calls=%async_computation.1 | async-start | bytes 2097152 | tf_op jit(solution)/shard_map/all_to_all | solution.py:355
  42.0 1.2 collective-permute-start
  43.3 6.8 %collective-permute-start.1 = (f32[32,128]{1,0:T(8,128)S(1)}, f32[32,128]{1,0:T(8,128)S(1)}, u32[]{:S(2)}, u32[]{:S(2)}) collective-permute-start(f32[32,128]{1,0:T(8,128)S(1)} %add.23), channel_id=1, source_target_pairs={{0,2},{1,3},{2,0},{3,1},{4,6},{5,7},{6,4},{7,5},{8,10},{9,11},{10,... | collective-permute-start | bytes 49160 | tf_op jit(solution)/shard_map/ppermute | solution.py:371
  50.1 4.6 %collective-permute-start.2 = (f32[32,128]{1,0:T(8,128)S(1)}, f32[32,128]{1,0:T(8,128)S(1)}, u32[]{:S(2)}, u32[]{:S(2)}) collective-permute-start(f32[32,128]{1,0:T(8,128)S(1)} %add.24), channel_id=1, source_target_pairs={{0,4},{1,5},{2,6},{3,7},{4,0},{5,1},{6,2},{7,3},{8,12},{9,13},{10,... | collective-permute-start | bytes 49160 | tf_op jit(solution)/shard_map/ppermute | solution.py:371
  54.7 5.4 %collective-permute-start.3 = (f32[32,128]{1,0:T(8,128)S(1)}, f32[32,128]{1,0:T(8,128)S(1)}, u32[]{:S(2)}, u32[]{:S(2)}) collective-permute-start(f32[32,128]{1,0:T(8,128)S(1)} %add.25), channel_id=1, source_target_pairs={{0,8},{1,9},{2,10},{3,11},{4,12},{5,13},{6,14},{7,15},{8,0},{9,1},... | collective-permute-start | bytes 49160 | tf_op jit(solution)/shard_map/ppermute | solution.py:371
  60.0 8.9 %collective-permute-start.4 = (f32[32,128]{1,0:T(8,128)S(1)}, f32[32,128]{1,0:T(8,128)S(1)}, u32[]{:S(2)}, u32[]{:S(2)}) collective-permute-start(f32[32,128]{1,0:T(8,128)S(1)} %add.26), channel_id=1, source_target_pairs={{0,16},{1,17},{2,18},{3,19},{4,20},{5,21},{6,22},{7,23},{8,24},{9,... | collective-permute-start | bytes 49160 | tf_op jit(solution)/shard_map/ppermute | solution.py:371
  69.0 2.2 %copy-start = (bf16[1024,2048]{1,0:T(8,128)(2,1)S(1)}, bf16[1024,2048]{1,0:T(8,128)(2,1)}, u32[]{:S(2)}) copy-start(bf16[1024,2048]{1,0:T(8,128)(2,1)} %keyval_w.1) | copy-start | bytes 12582916
  71.1 1.6 %copy-start.4 = (bf16[1024,1024]{1,0:T(8,128)(2,1)S(1)}, bf16[1024,1024]{1,0:T(8,128)(2,1)}, u32[]{:S(2)}) copy-start(bf16[1024,1024]{1,0:T(8,128)(2,1)} %out_w.3) | copy-start | bytes 6291460
  72.7 1.0 copy-start.19
  85.2 0.8 copy-start.21
  86.0 10.3 %copy-start.14 = (f32[1024]{0:T(1024)S(1)}, f32[1024]{0:T(1024)}, u32[]{:S(2)}) copy-start(f32[1024]{0:T(1024)} %param.27) | copy-start | bytes 12292
  86.0 10.3 %collective-permute-start.6 = (bf16[256,1024]{1,0:T(8,128)(2,1)S(1)}, bf16[256,1024]{1,0:T(8,128)(2,1)S(1)}, u32[]{:S(2)}, u32[]{:S(2)}) collective-permute-start(bf16[256,1024]{1,0:T(8,128)(2,1)S(1)} %get-tuple-element.14.norm_ref), channel_id=1, source_target_pairs={{1,0},{2,1},{3,2},{4,3},{5,4},{6,5},{7,6},{8,7},{9,8},{10,9},{11,1... | collective-permute-start | bytes 1572872 | tf_op jit(solution)/shard_map/ppermute | solution.py:404
  87.4 8.9 %collective-permute-start.5 = (bf16[256,1024]{1,0:T(8,128)(2,1)S(1)}, bf16[256,1024]{1,0:T(8,128)(2,1)S(1)}, u32[]{:S(2)}, u32[]{:S(2)}) collective-permute-start(bf16[256,1024]{1,0:T(8,128)(2,1)S(1)} %get-tuple-element.14.norm_ref), channel_id=1, source_target_pairs={{0,1},{1,2},{2,3},{3,4},{4,5},{5,6},{6,7},{7,8},{8,9},{9,10},{10,1... | collective-permute-start | bytes 1572872 | tf_op jit(solution)/shard_map/ppermute | solution.py:403
  96.3 2.2 %copy-start.1 = (bf16[1024,2048]{1,0:T(8,128)(2,1)S(1)}, bf16[1024,2048]{1,0:T(8,128)(2,1)}, u32[]{:S(2)}) copy-start(bf16[1024,2048]{1,0:T(8,128)(2,1)} %decode_w.1) | copy-start | bytes 12582916
  98.5 1.6 %copy-start.5 = (bf16[1024,1024]{1,0:T(8,128)(2,1)S(1)}, bf16[1024,1024]{1,0:T(8,128)(2,1)}, u32[]{:S(2)}) copy-start(bf16[1024,1024]{1,0:T(8,128)(2,1)} %out_w.4) | copy-start | bytes 6291460
  100.1 1.4 copy-start.20
  101.5 1.0 copy-start.22
  102.5 53.1 %copy-start.6 = (bf16[1024,1024]{1,0:T(8,128)(2,1)S(1)}, bf16[1024,1024]{1,0:T(8,128)(2,1)}, u32[]{:S(2)}) copy-start(bf16[1024,1024]{1,0:T(8,128)(2,1)} %out_w.5) | copy-start | bytes 6291460
where the time goes:
time: 159 us; the launch traced here: 158 us
  Pallas kernels  37.8 us (24%)
  waiting for transfers between devices  35.4 us (22%)
  blocking collectives  35.3 us (22%)
  starting transfers between devices  25 us (16%)
  local copies, waits for them, and re-layouts  18.9 us (12%)
  matrix products  5.77 us (4%)
    pallas_call x5, Pallas kernels, call(): pl.pallas_call(kernel, out_shape=[jax.ShapeDtypeStruct(shape, kind) for s...  37.8 us
    all_to_all x1, blocking collectives, exchange(): lax.all_to_all(rows.reshape(devices, capacity, features), AXES, split_axi...  35.3 us
    unnamed x48, local copies, waits for them, and re-layouts  18.9 us
    all_to_all x2, waiting for transfers between devices, exchange(): lax.all_to_all(rows.reshape(devices, capacity, features), AXES, split_axi...  18.1 us
    ppermute x5, waiting for transfers between devices, on_device(): lax.ppermute(counts, AXES, [(i, i ^ step) for i in range(devices)])  17.3 us
    all_to_all x2, starting transfers between devices, exchange(): lax.all_to_all(rows.reshape(devices, capacity, features), AXES, split_axi...  10.9 us
    ppermute x5, starting transfers between devices, on_device(): lax.ppermute(counts, AXES, [(i, i ^ step) for i in range(devices)])  9.54 us
    dot_general x1, matrix products, dot(): return jnp.dot(left, right, preferred_element_type=F32)  5.77 us
  transfers between devices with their start and end apart: 9, of which 6 were waited for; matrix products, arithmetic and copies ran while one was open for 4% of the time, Pallas kernels for 10%

commit v1 on v0

v1 whole, which is shorter than its diff:
```python
import functools

import jax
import jax.numpy as jnp
from jax import lax
from jax.experimental import pallas as pl
from jax.experimental.pallas import tpu as pltpu
from jax.sharding import PartitionSpec as P

HEADS = 16
BLOCK = 128
TILE = 512
LANES = 128
MASKED = -1e30
VMEM_MIB = 62
ENCODE_UNROLL = 1
PROCESS_UNROLL = 1
ANY, HBM, VMEM, SMEM = pl.ANY, pltpu.HBM, pltpu.VMEM, pltpu.SMEM
AXES = ("gx", "gy")
F32 = jnp.float32
BF16 = jnp.bfloat16
MIB = 1024 * 1024


def iota(shape, dim):
    return lax.broadcasted_iota(jnp.int32, shape, dim)


def floor_div(values, by):
    return jnp.floor((values.astype(F32) + 0.5) * (1.0 / by)).astype(jnp.int32)


def dot(left, right):
    return jnp.dot(left, right, preferred_element_type=F32)


def dot_t(left, right):
    return lax.dot_general(left, right, (((1,), (1,)), ((), ())), preferred_element_type=F32)


def dot_tl(left, right):
    return lax.dot_general(left, right, (((0,), (0,)), ((), ())), preferred_element_type=F32)


def normed(values, gain):
    wide = values.astype(F32)
    return wide * lax.rsqrt(jnp.mean(wide * wide, axis=-1, keepdims=True) + 1e-06) * gain


def block_hits(blocks, total_blocks):
    hits = iota((total_blocks, blocks.shape[1]), 0) == blocks
    return jnp.where(hits, 1.0, 0.0).astype(F32)


def block_counts(hits):
    counts = jnp.sum(hits, axis=1, keepdims=True)
    return jnp.broadcast_to(counts, (hits.shape[0], LANES)).astype(BF16)


def slots_of(hits, per_device, capacity):
    total_blocks, points = hits.shape
    earlier = jnp.where(iota((points, points), 0) < iota((points, points), 1), 1.0, 0.0)
    before = dot(hits.astype(BF16), earlier.astype(BF16))
    row, column = iota((total_blocks, total_blocks), 0), iota((total_blocks, total_blocks), 1)
    mates = (floor_div(row, per_device) == floor_div(column, per_device)) & (column < row)
    offset = dot(jnp.where(mates, 1.0, 0.0).astype(BF16), block_counts(hits))[:, :1]
    owner = floor_div(iota((total_blocks, 1), 0), per_device)
    base = owner.astype(F32) * capacity + offset
    return jnp.sum(hits * (base + before), axis=0, keepdims=True).astype(jnp.int32)


def placement(slot, slots):
    return jnp.where(iota((slots, slot.shape[1]), 0) == slot, 1.0, 0.0).astype(BF16)


class Fetch:
    def __init__(self, source, held, ready):
        self.copy = pltpu.make_async_copy(source, held, ready)
        self.held = held
        self.waiting = True
        self.copy.start()

    def __call__(self):
        if self.waiting:
            self.copy.wait()
            self.waiting = False
        return self.held


class Weight:
    def __init__(self, source, held, ready, base, count, first=0):
        self.source, self.held, self.ready, self.base, self.count = source, held, ready, base, count

        @pl.loop(0, count)
        def _(i):
            columns = pl.ds(pl.multiple_of((first + i) * TILE, TILE), TILE)
            pltpu.make_async_copy(source.at[:, columns], held.at[base + i], ready.at[base + i]).start()

    def product(self, rows, put):
        @pl.loop(0, self.count)
        def _(i):
            held = self.held.at[self.base + i]
            pltpu.make_async_copy(
                self.source.at[:, pl.ds(0, TILE)], held, self.ready.at[self.base + i]
            ).wait()
            put(pl.ds(pl.multiple_of(i * TILE, TILE), TILE), dot(rows[...], held[...]))


def store_in(ref):
    def put(columns, values):
        ref[:, columns] = values.astype(ref.dtype)

    return put


def count_lanes(encode_counts, decode_counts, devices, per_device):
    total_blocks = encode_counts.shape[0]
    lane = iota((devices, LANES), 1)
    labels = jnp.zeros((devices, LANES), F32)
    for kind, counts in enumerate((encode_counts, decode_counts)):
        for block in range(per_device):
            wanted = iota((devices, total_blocks), 0) * per_device + block
            wanted = jnp.where(iota((devices, total_blocks), 1) == wanted, 1.0, 0.0).astype(BF16)
            labels = labels + jnp.where(lane == kind * per_device + block, dot(wanted, counts), 0.0)
    return labels.astype(BF16)


def by_tiles(capacity):
    return capacity % 16 == 0


def fill_kernel(
    devices, per_device, capacity,
    state_hbm, encode_hbm, decode_hbm, gain_hbm, packed_ref,
    state_held, encode_held, decode_held, gain_held, ready,
):
    encode = Fetch(encode_hbm, encode_held, ready.at[0])
    decode = Fetch(decode_hbm, decode_held, ready.at[1])
    state = Fetch(state_hbm, state_held, ready.at[2])
    gain = Fetch(gain_hbm, gain_held, ready.at[3])
    total_blocks, slots = devices * per_device, devices * capacity
    encode_hits = block_hits(encode()[...], total_blocks)
    place = placement(slots_of(encode_hits, per_device, capacity), slots)
    decode_hits = block_hits(decode()[...], total_blocks)
    labels = count_lanes(block_counts(encode_hits), block_counts(decode_hits), devices, per_device)
    norm = normed(state()[...], gain()[...]).astype(BF16)
    features = norm.shape[1]
    if by_tiles(capacity):
        for tile in range(features // LANES):
            columns = dot(place, norm[:, tile * LANES : (tile + 1) * LANES]).astype(BF16)
            packed_ref[:, pl.ds(tile * capacity, capacity), :] = columns.reshape(devices, capacity, LANES)
        last = pl.ds(features // LANES * capacity, 8)
        packed_ref[:, last, :] = jnp.broadcast_to(labels[:, None, :], (devices, 8, LANES))
    else:
        packed_ref[:, pl.ds(0, features)] = dot(place, norm).astype(BF16)
        owner = floor_div(iota((slots, devices), 0), capacity) == iota((slots, devices), 1)
        packed_ref[:, pl.ds(features, LANES)] = dot(jnp.where(owner, 1.0, 0.0).astype(BF16), labels).astype(BF16)


def query_kernel(
    devices, per_device, capacity, scale,
    mesh_hbm, mesh_gain_hbm, encode_w, grid_hbm, grid_gain_hbm, decode_w, decode_hbm,
    query_ref, packed_ref,
    mesh_held, mesh_gain_held, grid_held, grid_gain_held, decode_held, ready,
    norm_ref, weights, arrived,
):
    decode = Fetch(decode_hbm, decode_held, ready.at[0])
    grid = Fetch(grid_hbm, grid_held, ready.at[1])
    grid_gain = Fetch(grid_gain_hbm, grid_gain_held, ready.at[2])
    mesh = Fetch(mesh_hbm, mesh_held, ready.at[3])
    mesh_gain = Fetch(mesh_gain_hbm, mesh_gain_held, ready.at[4])
    count = encode_w.shape[1] // TILE
    decode_weight = Weight(decode_w, weights, arrived, 0, count)
    encode_weight = Weight(encode_w, weights, arrived, count, count)
    slots = packed_ref.shape[0]
    hits = block_hits(decode()[...], devices * per_device)
    place = placement(slots_of(hits, per_device, capacity), slots)
    norm_ref[...] = normed(grid()[...], grid_gain()[...]).astype(BF16)

    def put_packed(columns, values):
        rounded = (values.astype(BF16).astype(F32) * scale).astype(BF16)
        packed_ref[:, columns] = dot(place, rounded).astype(BF16)

    decode_weight.product(norm_ref, put_packed)
    norm_ref[...] = normed(mesh()[...], mesh_gain()[...]).astype(BF16)

    def put_query(columns, values):
        query_ref[:, columns] = (values.astype(BF16).astype(F32) * scale).astype(BF16)

    encode_weight.product(norm_ref, put_query)


def lanes_of(labels, first, count):
    row, lane = iota((8, LANES), 0), iota((8, LANES), 1)
    wanted = (lane == row + first) & (row < count)
    return dot_t(jnp.where(wanted, 1.0, 0.0).astype(BF16), labels).astype(BF16)


def even_lanes(shape, head_size):
    return iota(shape, len(shape) - 1) < head_size


def split_heads(values, head_size):
    even = even_lanes(values.shape, head_size)
    zero = jnp.zeros_like(values)
    return jnp.concatenate([jnp.where(even, values, zero), jnp.where(even, zero, values)], axis=0)


def join_heads(values, head_size):
    rows = values.shape[0] // 2
    even = even_lanes((rows, values.shape[1]), head_size)
    return jnp.where(even, values[:rows], values[rows:])


def encode_kernel(
    per_device, capacity, head_size, unroll,
    received_hbm, query_hbm, mesh_hbm, gain_hbm, keyval_w, out_w,
    mid_ref, norm_ref, labels_ref,
    received_held, query_held, mesh_held, gain_held, ready,
    rows_ref, keyval, attended, bias, weights, arrived,
):
    features = mid_ref.shape[1]
    devices = labels_ref.shape[0]
    slots = devices * capacity
    kv_count, out_count = keyval_w.shape[1] // TILE, features // TILE
    received = Fetch(received_hbm, received_held, ready.at[0])
    keyval_weight = Weight(keyval_w, weights, arrived, 0, kv_count)
    query_rows = Fetch(query_hbm, query_held, ready.at[1])
    out_weight = Weight(out_w, weights, arrived, kv_count, out_count)
    mesh = Fetch(mesh_hbm, mesh_held, ready.at[2])
    gain = Fetch(gain_hbm, gain_held, ready.at[3])
    received_ref = received()
    if by_tiles(capacity):
        for tile in range(features // LANES):
            part = received_ref[:, pl.ds(tile * capacity, capacity), :]
            rows_ref[:, pl.ds(tile * LANES, LANES)] = part.reshape(slots, LANES)
        last = received_ref[:, pl.ds(features // LANES * capacity, 8), :]
        labels = jnp.max(last.astype(F32), axis=1).astype(BF16)
        rows = rows_ref
    else:
        rows = received_ref.at[:, pl.ds(0, features)]
        first = iota((devices, slots), 1) == iota((devices, slots), 0) * capacity
        labels = dot(jnp.where(first, 1.0, 0.0).astype(BF16), received_ref[:, pl.ds(features, LANES)]).astype(BF16)
    labels_ref[...] = labels
    keyval_weight.product(rows, store_in(keyval))

    sender = floor_div(iota((devices, slots), 1), capacity) == iota((devices, slots), 0)
    filled = dot(lanes_of(labels, 0, per_device), jnp.where(sender, 1.0, 0.0).astype(BF16))
    lane = iota((1, slots), 1)
    place = (lane - floor_div(lane, capacity) * capacity).astype(F32)
    begin = jnp.zeros((1, slots), F32)
    for block in range(per_device):
        end = begin + filled[block : block + 1]
        bias[block : block + 1] = jnp.where((place >= begin) & (place < end), 0.0, MASKED)
        begin = end
    query_ref = query_rows()

    @pl.loop(0, features // LANES, unroll=unroll)
    def _(pair):
        columns = pl.ds(pl.multiple_of(pair * LANES, LANES), LANES)
        value_columns = pl.ds(pl.multiple_of(features + pair * LANES, LANES), LANES)
        keys, values = keyval[:, columns], keyval[:, value_columns]
        for block in range(per_device):
            block_rows = pl.ds(block * BLOCK, BLOCK)
            queries = split_heads(query_ref[block_rows, columns], head_size)
            scores = dot_t(queries, keys) + bias[block : block + 1]
            powers = jnp.exp(scores - jnp.max(scores, axis=-1, keepdims=True))
            sums = jnp.sum(powers, axis=-1, keepdims=True)
            output = dot(powers.astype(BF16), values) / sums
            attended[block_rows, columns] = join_heads(output, head_size).astype(BF16)

    mesh_ref = mesh()

    def put_mid(columns, values):
        mid_ref[:, columns] = (mesh_ref[:, columns].astype(F32) + values).astype(BF16)

    out_weight.product(attended, put_mid)
    norm_ref[...] = normed(mid_ref[...], gain()[...]).astype(BF16)


def own_kernel(scale, norm_hbm, qkv_w, qkv_ref, norm_held, ready, weights, arrived):
    features = norm_hbm.shape[1]
    norm = Fetch(norm_hbm, norm_held, ready.at[0])
    weight = Weight(qkv_w, weights, arrived, 0, qkv_w.shape[1] // TILE)
    tiles = features // TILE

    def put(columns, values):
        qkv_ref[:, columns] = values.astype(BF16)

    weight.product(norm(), put)
    queries = pl.ds(0, features)
    qkv_ref[:, queries] = (qkv_ref[:, queries].astype(F32) * scale).astype(BF16)


def process_kernel(
    per_device, capacity, head_size, unroll,
    me_ref, position_ref, first_hbm, norm_hbm, second_hbm, qkv_hbm, mid_hbm, queries_hbm, gain_hbm, labels_hbm,
    qkv_w, out_w, decode_w,
    answers_ref,
    qkv_held, mid_held, queries_held, gain_held, labels_held, ready, picked,
    chosen, other, attended, mesh_out, weights, arrived,
):
    features = mid_hbm.shape[1]
    slots, devices = queries_hbm.shape[0], labels_hbm.shape[0]
    tiles = features // TILE
    odd = me_ref[0] % 2
    for block in range(per_device):
        rows = pl.ds(block * BLOCK, BLOCK)
        position = position_ref[block]
        sides = ((first_hbm, 2 * (1 - odd)), (norm_hbm, 1), (second_hbm, 2 * odd))
        for source, side in sides:
            for place in range(per_device):
                @pl.when(position == side * per_device + place)
                def _():
                    block_rows = source.at[pl.ds(place * BLOCK, BLOCK)]
                    pltpu.make_async_copy(block_rows, chosen.at[rows], picked.at[block]).start()

    kv_weight = Weight(qkv_w, weights, arrived, 0, 2 * tiles, tiles)
    out_weight = Weight(out_w, weights, arrived, 2 * tiles, tiles)
    decode_weight = Weight(decode_w, weights, arrived, 3 * tiles, 2 * tiles)
    qkv = Fetch(qkv_hbm, qkv_held, ready.at[0])
    mid = Fetch(mid_hbm, mid_held, ready.at[1])
    queries_rows = Fetch(queries_hbm, queries_held, ready.at[2])
    gain = Fetch(gain_hbm, gain_held, ready.at[3])
    labels = Fetch(labels_hbm, labels_held, ready.at[4])
    for block in range(per_device):
        rows = pl.ds(block * BLOCK, BLOCK)
        pltpu.make_async_copy(norm_hbm.at[rows], chosen.at[rows], picked.at[block]).wait()
    kv_weight.product(chosen, store_in(other))
    qkv_ref = qkv()

    @pl.loop(0, features // LANES, unroll=unroll)
    def _(pair):
        columns = pl.ds(pl.multiple_of(pair * LANES, LANES), LANES)
        second = pl.ds(pl.multiple_of(features + pair * LANES, LANES), LANES)
        third = pl.ds(pl.multiple_of(2 * features + pair * LANES, LANES), LANES)
        for block in range(per_device):
            rows = pl.ds(block * BLOCK, BLOCK)
            queries = split_heads(qkv_ref[rows, columns], head_size)
            keys = jnp.concatenate([qkv_ref[rows, second], other[rows, columns]], axis=0)
            values = jnp.concatenate([qkv_ref[rows, third], other[rows, second]], axis=0)
            scores = dot_t(queries, keys)
            powers = jnp.exp(scores - jnp.max(scores, axis=-1, keepdims=True))
            sums = jnp.sum(powers, axis=-1, keepdims=True)
            output = dot(powers.astype(BF16), values) / sums
            attended[rows, columns] = join_heads(output, head_size).astype(BF16)

    mid_ref = mid()

    def put_out(columns, values):
        mesh_out[:, columns] = (mid_ref[:, columns].astype(F32) + values).astype(BF16)

    out_weight.product(attended, put_out)
    chosen[...] = normed(mesh_out[...], gain()[...]).astype(BF16)
    decode_weight.product(chosen, store_in(other))

    sender = floor_div(iota((slots, devices), 0), capacity) == iota((slots, devices), 1)
    filled = dot_t(jnp.where(sender, 1.0, 0.0).astype(BF16), lanes_of(labels()[...], per_device, per_device))
    row = iota((slots, 1), 0)
    place = (row - floor_div(row, capacity) * capacity).astype(F32)
    reads, begin = [], jnp.zeros((slots, 1), F32)
    for block in range(per_device):
        end = begin + filled[:, block : block + 1]
        here = jnp.where((place >= begin) & (place < end), 1.0, 0.0)
        reads.append(jnp.broadcast_to(here, (slots, BLOCK)))
        begin = end
    queries_ref = queries_rows()

    @pl.loop(0, features // LANES, unroll=unroll)
    def _(pair):
        columns = pl.ds(pl.multiple_of(pair * LANES, LANES), LANES)
        second = pl.ds(pl.multiple_of(features + pair * LANES, LANES), LANES)
        queries = queries_ref[:, columns]
        even = even_lanes((slots, LANES), head_size)
        outputs = []
        for head in range(LANES // head_size):
            picked = jnp.where(even if head == 0 else ~even, queries, jnp.zeros_like(queries))
            scores = dot_t(picked, other[:, columns])
            chosen_scores = scores[:, :BLOCK]
            for block in range(1, per_device):
                here = scores[:, block * BLOCK : (block + 1) * BLOCK]
                chosen_scores = jnp.where(reads[block] > 0.5, here, chosen_scores)
            powers = jnp.exp(chosen_scores - jnp.max(chosen_scores, axis=-1, keepdims=True))
            sums = jnp.sum(powers, axis=-1, keepdims=True)
            spread = jnp.concatenate(
                [jnp.where(reads[block] > 0.5, powers, 0.0).astype(BF16) for block in range(per_device)], axis=1
            )
            outputs.append(dot(spread, other[:, second]) / sums)
        answers_ref[:, columns] = jnp.where(even, outputs[0], outputs[1]).astype(BF16)


def unpack_kernel(
    devices, per_device, capacity, replies_hbm, decode_hbm, out_w, update_ref,
    decode_held, replies_held, ready, decoded, weights, arrived,
):
    decode = Fetch(decode_hbm, decode_held, ready.at[0])
    replies = Fetch(replies_hbm, replies_held, ready.at[1])
    weight = Weight(out_w, weights, arrived, 0, out_w.shape[1] // TILE)
    hits = block_hits(decode()[...], devices * per_device)
    place = placement(slots_of(hits, per_device, capacity), replies_hbm.shape[0])
    decoded[...] = dot_tl(place, replies()[...]).astype(BF16)
    weight.product(decoded, store_in(update_ref))


def call(kernel, operands, outs, scratch, name, flops):
    return pl.pallas_call(
        kernel,
        out_shape=[jax.ShapeDtypeStruct(shape, kind) for shape, kind in outs],
        in_specs=[pl.BlockSpec(memory_space=space) for space, _ in operands],
        out_specs=[pl.BlockSpec(memory_space=VMEM) for _ in outs],
        scratch_shapes=scratch,
        name=name,
        cost_estimate=pl.CostEstimate(flops=flops, bytes_accessed=4 * MIB, transcendentals=0),
        compiler_params=pltpu.CompilerParams(vmem_limit_bytes=VMEM_MIB * MIB),
    )(*[value for _, value in operands])


def held_like(*values):
    return [*[VMEM(value.shape, value.dtype) for value in values], pltpu.SemaphoreType.DMA((len(values),))]


def weights_held(count, features):
    return [VMEM((count, features, TILE), BF16), pltpu.SemaphoreType.DMA((count,))]


def on_device(
    grid_state,
    mesh_state,
    encode_block,
    neighbour_block,
    decode_block,
    encode_grid_gain,
    encode_mesh_gain,
    process_gain,
    decode_grid_gain,
    decode_mesh_gain,
    encode_query,
    encode_keyval,
    encode_out,
    process_qkv,
    process_out,
    decode_query,
    decode_keyval,
    decode_out,
):
    devices = lax.axis_size(AXES)
    me = lax.axis_index(AXES)
    grid_count, features = grid_state.shape
    mesh_rows = mesh_state.shape[0]
    per_device = mesh_rows // BLOCK
    total_blocks = per_device * devices
    capacity = max(4, 2 * grid_count // devices)
    slots = devices * capacity
    head_size = features // HEADS
    scale = head_size ** (-0.5)
    tiles = features // TILE
    me_row = me.astype(jnp.int32).reshape(1)
    position = neighbour_block - me * per_device + per_device
    encode_row, decode_row = encode_block.reshape(1, -1), decode_block.reshape(1, -1)
    encode_grid_gain, encode_mesh_gain, process_gain, decode_grid_gain, decode_mesh_gain = [
        gain.reshape(1, -1)
        for gain in (encode_grid_gain, encode_mesh_gain, process_gain, decode_grid_gain, decode_mesh_gain)
    ]

    def exchange(rows, *shape):
        return lax.all_to_all(rows.reshape(devices, *shape), AXES, split_axis=0, concat_axis=0, tiled=True)

    if by_tiles(capacity):
        payload = (capacity * features // LANES + 8, LANES)
        packed_shape = (devices, *payload)
    else:
        payload = (capacity, features + LANES)
        packed_shape = (slots, features + LANES)
    (packed,) = call(
        functools.partial(fill_kernel, devices, per_device, capacity),
        [(HBM, grid_state), (HBM, encode_row), (HBM, decode_row), (HBM, encode_grid_gain)],
        [(packed_shape, BF16)],
        held_like(grid_state, encode_row, decode_row, encode_grid_gain),
        "fill",
        flops=600_000_000,
    )
    received = exchange(packed, *payload).reshape(packed_shape)
    query, packed_queries = call(
        functools.partial(query_kernel, devices, per_device, capacity, scale),
        [
            (HBM, mesh_state), (HBM, encode_mesh_gain), (HBM, encode_query),
            (HBM, grid_state), (HBM, decode_grid_gain), (HBM, decode_query), (HBM, decode_row),
        ],
        [((mesh_rows, features), BF16), ((slots, features), BF16)],
        [
            *held_like(mesh_state, encode_mesh_gain, grid_state, decode_grid_gain, decode_row),
            VMEM((grid_count, features), BF16),
            *weights_held(2 * tiles, features),
        ],
        "queries",
        flops=2_000_000_000,
    )
    arrived_queries = exchange(packed_queries, capacity, features).reshape(slots, features)
    mesh_mid, process_norm, labels = call(
        functools.partial(encode_kernel, per_device, capacity, head_size, ENCODE_UNROLL),
        [
            (ANY, received), (HBM, query), (HBM, mesh_state), (HBM, process_gain),
            (HBM, encode_keyval), (HBM, encode_out),
        ],
        [((mesh_rows, features), BF16), ((mesh_rows, features), BF16), ((devices, LANES), BF16)],
        [
            *held_like(received, query, mesh_state, process_gain),
            VMEM((slots, features), BF16),
            VMEM((slots, 2 * features), BF16),
            VMEM((mesh_rows, features), BF16),
            VMEM((8, slots), F32),
            *weights_held(3 * tiles, features),
        ],
        "encode",
        flops=5_000_000_000,
    )
    pairs = [(i, i ^ 1) for i in range(devices)]
    across = [(i, i + 1 if i % 2 else i - 1) for i in range(1, devices - 1)]
    first = lax.ppermute(process_norm, AXES, pairs)
    second = lax.ppermute(process_norm, AXES, across)
    (mesh_qkv,) = call(
        functools.partial(own_kernel, scale),
        [(HBM, process_norm), (HBM, process_qkv)],
        [((mesh_rows, 3 * features), BF16)],
        [*held_like(process_norm), *weights_held(3 * tiles, features)],
        "own",
        flops=2_000_000_000,
    )
    (answers,) = call(
        functools.partial(process_kernel, per_device, capacity, head_size, PROCESS_UNROLL),
        [
            (SMEM, me_row), (SMEM, position), (ANY, first), (HBM, process_norm), (ANY, second), (HBM, mesh_qkv),
            (HBM, mesh_mid), (ANY, arrived_queries), (HBM, decode_mesh_gain), (HBM, labels),
            (HBM, process_qkv), (HBM, process_out), (HBM, decode_keyval),
        ],
        [((slots, features), BF16)],
        [
            *held_like(mesh_qkv, mesh_mid, arrived_queries, decode_mesh_gain, labels),
            pltpu.SemaphoreType.DMA((per_device,)),
            VMEM((mesh_rows, features), BF16),
            VMEM((mesh_rows, 2 * features), BF16),
            VMEM((mesh_rows, features), BF16),
            VMEM((mesh_rows, features), BF16),
            *weights_held(5 * tiles, features),
        ],
        "process",
        flops=6_000_000_000,
    )
    replies = exchange(answers, capacity, features).reshape(slots, features)
    (update,) = call(
        functools.partial(unpack_kernel, devices, per_device, capacity),
        [(ANY, replies), (HBM, decode_row), (HBM, decode_out)],
        [((grid_count, features), BF16)],
        [*held_like(decode_row, replies), VMEM((grid_count, features), BF16), *weights_held(tiles, features)],
        "unpack",
        flops=1_000_000_000,
    )
    return update


def solution(mesh):
    in_specs = (P(AXES, None), P(AXES, None), P(AXES), P(AXES), P(AXES), *[P()] * 13)
    return jax.shard_map(
        on_device, mesh=mesh, in_specs=in_specs, out_specs=P(AXES, None), check_vma=False
    )
```

time: 159 us -> 130 us (0.82)
  local copies, waits for them, and re-layouts: 18.9 us -> 0.96 us
  Pallas kernels: 37.8 us -> 50.7 us
  starting transfers between devices: 25 us -> 14.9 us
  waiting for transfers between devices: 35.4 us -> 26.1 us
  matrix products: 5.77 us -> 0 us
    unnamed x48 -> x8, local copies, waits for them, and re-layouts: 18.9 us -> 0.96 us
    ppermute x7 -> x2, waiting for transfers between devices: 17.3 us -> 0.01 us  [the longest x1 0.01 us: on_device(): second = lax.ppermute(process_norm, AXES, across)]
    pallas_call x5 -> x6, Pallas kernels: 37.8 us -> 50.7 us  [call(): pl.pallas_call(kernel, out_shape=[jax.ShapeDtypeStruct(shape, kind) for s...]
    ppermute x7 -> x2, starting transfers between devices: 14 us -> 3.79 us  [the longest x1 3.09 us: on_device(): first = lax.ppermute(process_norm, AXES, pairs)]
    all_to_all x2, waiting for transfers between devices: 18.1 us -> 26.1 us  [exchange(): lax.all_to_all(rows.reshape(devices, *shape), AXES, split_axis=0, concat_...]
    dot_general x1 -> x0, matrix products: 5.77 us -> none  [dot(): return jnp.dot(left, right, preferred_element_type=F32)]
  transfers between devices with their start and end apart: 9 -> 4, of which waited for: 6 -> 2; matrix products, arithmetic and copies ran while one was open for 4% -> 0% of each run, Pallas kernels for 10% -> 18%
where the time goes in v1:
time: 130 us
  Pallas kernels  50.7 us (39%)
  blocking collectives  36.4 us (28%)
  waiting for transfers between devices  26.1 us (20%)
  starting transfers between devices  14.9 us (11%)
    pallas_call x6, Pallas kernels, call(): pl.pallas_call(kernel, out_shape=[jax.ShapeDtypeStruct(shape, kind) for s...  50.7 us
    all_to_all x1, blocking collectives, exchange(): lax.all_to_all(rows.reshape(devices, *shape), AXES, split_axis=0, concat_...  36.4 us
    all_to_all x2, waiting for transfers between devices, exchange(): lax.all_to_all(rows.reshape(devices, *shape), AXES, split_axis=0, concat_...  26.1 us
    all_to_all x2, starting transfers between devices, exchange(): lax.all_to_all(rows.reshape(devices, *shape), AXES, split_axis=0, concat_...  11.1 us
    ppermute x1, starting transfers between devices, on_device(): first = lax.ppermute(process_norm, AXES, pairs)  3.09 us
  transfers between devices with their start and end apart: 4, of which 2 were waited for; matrix products, arithmetic and copies ran while one was open for 0% of the time, Pallas kernels for 18%

profile of v1, /device:TPU:0, one launch (start us, length us, event | category | flops | bytes accessed | tf_op | source)
XLA Modules:
  0.0 129.7 jit_solution(4929072113661740675)
XLA Ops:
  0.0 3.2 %fill.1 = bf16[32,136,128]{2,1,0:T(8,128)(2,1)} custom-call(bf16[256,1024]{1,0:T(8,128)(2,1)} %grid_hbm.1, s32[1,256]{1,0:T(1,128)} %bitcast.20, s32[1,256]{1,0:T(1,128)} %bitcast.21, f32[1,1024]{1,0:T(1,128)} %bitcast.15), custom_call_target="tpu_custom_call" | custom-call | flops 600000000 | bytes 4194304 | tf_op jit(solution)/shard_map/fill/pallas_call | solution.py:406
  3.2 7.3 %all-to-all-start = ((bf16[32,136,128]{2,1,0:T(8,128)(2,1)}), bf16[32,136,128]{2,1,0:T(8,128)(2,1)S(1)}, u32[]{:S(2)}, u32[]{:S(2)}) async-start(bf16[32,136,128]{2,1,0:T(8,128)(2,1)} %fill.1), calls=%async_computation | async-start | bytes 2228224 | tf_op jit(solution)/shard_map/all_to_all | solution.py:466
  10.5 5.0 %queries.1 = (bf16[256,1024]{1,0:T(8,128)(2,1)}, bf16[512,1024]{1,0:T(8,128)(2,1)}) custom-call(bf16[256,1024]{1,0:T(8,128)(2,1)} %mesh_hbm.3, f32[1,1024]{1,0:T(1,128)} %bitcast.16, bf16[1024,1024]{1,0:T(8,128)(2,1)} %encode_w.1, bf16[256,1024]{1,0:T(8,128)(2,1)} %grid_hbm.1, f32[1,1024]{1,0:T(1,128)} %bitcast.17, bf16[1024,1024]{1,0:T(8,128)(2,1)} %decode_w.2, ...), custom_call_target="tpu_custom_call" | custom-call | flops 2000000000 | bytes 4194304 | tf_op jit(solution)/shard_map/queries/pallas_call | solution.py:406
  15.6 22.6 %all-to-all-done.received_hbm = bf16[32,136,128]{2,1,0:T(8,128)(2,1)S(1)} async-done(((bf16[32,136,128]{2,1,0:T(8,128)(2,1)}), bf16[32,136,128]{2,1,0:T(8,128)(2,1)S(1)}, u32[]{:S(2)}, u32[]{:S(2)}) %all-to-all-start) | async-done | bytes 1114144 | tf_op jit(solution)/shard_map/all_to_all | solution.py:466
  38.2 0.0 copy-start
  38.2 3.7 %all-to-all-start.1 = ((bf16[32,16,1024]{2,1,0:T(8,128)(2,1)}), bf16[32,16,1024]{2,1,0:T(8,128)(2,1)}, u32[]{:S(2)}, u32[]{:S(2)}) async-start(bf16[32,16,1024]{2,1,0:T(8,128)(2,1)} %bitcast.12), calls=%async_computation.1 | async-start | bytes 2097152 | tf_op jit(solution)/shard_map/all_to_all | solution.py:466
  41.9 0.0 copy-done
  41.9 0.0 copy-start.3
  41.9 13.0 %encode.1 = (bf16[256,1024]{1,0:T(8,128)(2,1)}, bf16[256,1024]{1,0:T(8,128)(2,1)}, bf16[32,128]{1,0:T(8,128)(2,1)}) custom-call(bf16[32,136,128]{2,1,0:T(8,128)(2,1)} %copy-done, bf16[256,1024]{1,0:T(8,128)(2,1)} %get-tuple-element.10.query_hbm, bf16[256,1024]{1,0:T(8,128)(2,1)} %mesh_hbm.3, f32[1,1024]{1,0:T(1,128)} %bitcast.18, ...), custom_call_target="tpu_custom_call" | custom-call | flops 5000000000 | bytes 4194304 | tf_op jit(solution)/shard_map/encode/pallas_call | solution.py:406
  54.9 0.7 collective-permute-start.1
  55.6 3.1 %collective-permute-start = (bf16[256,1024]{1,0:T(8,128)(2,1)}, bf16[256,1024]{1,0:T(8,128)(2,1)S(1)}, u32[]{:S(2)}, u32[]{:S(2)}) collective-permute-start(bf16[256,1024]{1,0:T(8,128)(2,1)} %get-tuple-element.11.norm_hbm), channel_id=1, source_target_pairs={{0,1},{1,0},{2,3},{3,2},{4,5},{5,4},{6,7},{7,6},{8,9},{9,8},{10,11... | collective-permute-start | bytes 1572872 | tf_op jit(solution)/shard_map/ppermute | solution.py:519
  58.7 0.0 copy-done.3
  58.7 0.5 subtract_add_fusion.position_ref
  59.2 5.3 %own.1.qkv_hbm = bf16[256,3072]{1,0:T(8,128)(2,1)} custom-call(bf16[256,1024]{1,0:T(8,128)(2,1)} %get-tuple-element.11.norm_hbm, bf16[1024,3072]{1,0:T(8,128)(2,1)} %qkv_w.3), custom_call_target="tpu_custom_call" | custom-call | flops 2000000000 | bytes 4194304 | tf_op jit(solution)/shard_map/own/pallas_call | solution.py:406
  64.6 3.5 %all-to-all-done.1 = bf16[32,16,1024]{2,1,0:T(8,128)(2,1)} async-done(((bf16[32,16,1024]{2,1,0:T(8,128)(2,1)}), bf16[32,16,1024]{2,1,0:T(8,128)(2,1)}, u32[]{:S(2)}, u32[]{:S(2)}) %all-to-all-start.1) | async-done | bytes 1048608 | tf_op jit(solution)/shard_map/all_to_all | solution.py:466
  68.1 0.0 collective-permute-done.1.second_hbm
  68.1 0.0 copy-start.1
  68.1 0.0 collective-permute-done.first_hbm
  68.1 0.0 copy-start.2
  68.1 0.8 copy-done.1
  68.9 0.2 copy-done.2
  69.1 20.8 %process.1 = bf16[512,1024]{1,0:T(8,128)(2,1)} custom-call(s32[1]{0:T(128)} %bitcast.me_ref, s32[2]{0:T(128)} %subtract_add_fusion.position_ref, bf16[256,1024]{1,0:T(8,128)(2,1)} %copy-done.2, bf16[256,1024]{1,0:T(8,128)(2,1)} %get-tuple-element.11.norm_hbm, bf16[256,1024]{1,0:T(8,128)(2,1)} %copy-done.1, bf16[256,3072]{1,0:T(8,128)(2,1)} %own.1.qkv_hbm, ...), custom_call_target="tpu_custom_call" | custom-call | flops 6000000000 | bytes 4194304 | tf_op jit(solution)/shard_map/process/pallas_call | solution.py:406
  89.9 36.4 %all_to_all.15 = bf16[32,16,1024]{2,1,0:T(8,128)(2,1)} all-to-all(bf16[32,16,1024]{2,1,0:T(8,128)(2,1)} %bitcast.13), channel_id=1, replica_groups=mesh['gx'=4,'gy'=8] {'gx','gy'}, dimensions={0} | all-to-all | bytes 2097152 | tf_op jit(solution)/shard_map/all_to_all | solution.py:466
  126.2 3.4 %unpack.1 = bf16[256,1024]{1,0:T(8,128)(2,1)} custom-call(bf16[512,1024]{1,0:T(8,128)(2,1)} %bitcast.14, s32[1,256]{1,0:T(1,128)} %bitcast.23, bf16[1024,1024]{1,0:T(8,128)(2,1)} %out_w.5), custom_call_target="tpu_custom_call" | custom-call | flops 1000000000 | bytes 4194304 | tf_op jit(solution)/shard_map/unpack/pallas_call | solution.py:406
Async XLA Ops:
  3.2 34.9 %all-to-all-start = ((bf16[32,136,128]{2,1,0:T(8,128)(2,1)}), bf16[32,136,128]{2,1,0:T(8,128)(2,1)S(1)}, u32[]{:S(2)}, u32[]{:S(2)}) async-start(bf16[32,136,128]{2,1,0:T(8,128)(2,1)} %fill.1), calls=%async_computation | async-start | bytes 2228224 | tf_op jit(solution)/shard_map/all_to_all | solution.py:466
  38.2 3.8 %copy-start = (bf16[32,136,128]{2,1,0:T(8,128)(2,1)}, bf16[32,136,128]{2,1,0:T(8,128)(2,1)S(1)}, u32[]{:S(2)}) copy-start(bf16[32,136,128]{2,1,0:T(8,128)(2,1)S(1)} %all-to-all-done.received_hbm) | copy-start | bytes 3342340
  38.2 29.9 %all-to-all-start.1 = ((bf16[32,16,1024]{2,1,0:T(8,128)(2,1)}), bf16[32,16,1024]{2,1,0:T(8,128)(2,1)}, u32[]{:S(2)}, u32[]{:S(2)}) async-start(bf16[32,16,1024]{2,1,0:T(8,128)(2,1)} %bitcast.12), calls=%async_computation.1 | async-start | bytes 2097152 | tf_op jit(solution)/shard_map/all_to_all | solution.py:466
  41.9 16.8 %copy-start.3 = (s32[2]{0:T(128)S(1)}, s32[2]{0:T(128)}, u32[]{:S(2)}) copy-start(s32[2]{0:T(128)} %param.21) | copy-start | bytes 28
  54.9 13.2 %collective-permute-start.1 = (bf16[256,1024]{1,0:T(8,128)(2,1)}, bf16[256,1024]{1,0:T(8,128)(2,1)S(1)}, u32[]{:S(2)}, u32[]{:S(2)}) collective-permute-start(bf16[256,1024]{1,0:T(8,128)(2,1)} %get-tuple-element.11.norm_hbm), channel_id=1, source_target_pairs={{1,2},{2,1},{3,4},{4,3},{5,6},{6,5},{7,8},{8,7},{9,10},{10,9},{11,... | collective-permute-start | bytes 1572872 | tf_op jit(solution)/shard_map/ppermute | solution.py:520
  55.6 12.5 %collective-permute-start = (bf16[256,1024]{1,0:T(8,128)(2,1)}, bf16[256,1024]{1,0:T(8,128)(2,1)S(1)}, u32[]{:S(2)}, u32[]{:S(2)}) collective-permute-start(bf16[256,1024]{1,0:T(8,128)(2,1)} %get-tuple-element.11.norm_hbm), channel_id=1, source_target_pairs={{0,1},{1,0},{2,3},{3,2},{4,5},{5,4},{6,7},{7,6},{8,9},{9,8},{10,11... | collective-permute-start | bytes 1572872 | tf_op jit(solution)/shard_map/ppermute | solution.py:519
  68.1 0.8 copy-start.1
  68.1 1.0 copy-start.2

commit v2 on v1

--- a/solution.py
+++ b/solution.py
@@ -12,9 +12,10 @@
 TILE = 512
 LANES = 128
 MASKED = -1e30
-VMEM_MIB = 62
-ENCODE_UNROLL = 1
-PROCESS_UNROLL = 1
+VMEM_MIB = 56
+ENCODE_UNROLL = 4
+PROCESS_UNROLL = 8
+DECODE_UNROLL = 8
 ANY, HBM, VMEM, SMEM = pl.ANY, pltpu.HBM, pltpu.VMEM, pltpu.SMEM
 AXES = ("gx", "gy")
 F32 = jnp.float32
@@ -88,22 +89,37 @@
 
 
 class Weight:
-    def __init__(self, source, held, ready, base, count, first=0):
+    def __init__(self, source, held, ready, base, count, first=0, semaphore=None):
+        semaphore = base if semaphore is None else semaphore
         self.source, self.held, self.ready, self.base, self.count = source, held, ready, base, count
+        self.semaphore = semaphore
 
         @pl.loop(0, count)
         def _(i):
             columns = pl.ds(pl.multiple_of((first + i) * TILE, TILE), TILE)
-            pltpu.make_async_copy(source.at[:, columns], held.at[base + i], ready.at[base + i]).start()
+            pltpu.make_async_copy(source.at[:, columns], held.at[base + i], ready.at[semaphore + i]).start()
+
+    def arrive(self, i):
+        held = self.held.at[self.base + i]
+        pltpu.make_async_copy(self.source.at[:, pl.ds(0, TILE)], held, self.ready.at[self.semaphore + i]).wait()
+        return held
+
+    def wait(self):
+        @pl.loop(0, self.count)
+        def _(i):
+            self.arrive(i)
 
     def product(self, rows, put):
         @pl.loop(0, self.count)
         def _(i):
-            held = self.held.at[self.base + i]
-            pltpu.make_async_copy(
-                self.source.at[:, pl.ds(0, TILE)], held, self.ready.at[self.base + i]
-            ).wait()
+            held = self.arrive(i)
             put(pl.ds(pl.multiple_of(i * TILE, TILE), TILE), dot(rows[...], held[...]))
+
+
+def product(rows, held, put):
+    @pl.loop(0, held.shape[0])
+    def _(i):
+        put(pl.ds(pl.multiple_of(i * TILE, TILE), TILE), dot(rows[...], held[i]))
 
 
 def store_in(ref):
@@ -278,35 +294,49 @@
     norm_ref[...] = normed(mid_ref[...], gain()[...]).astype(BF16)
 
 
-def own_kernel(scale, norm_hbm, qkv_w, qkv_ref, norm_held, ready, weights, arrived):
+def own_kernel(scale, norm_hbm, qkv_w, qkv_ref, norm_held, ready, qkv_held, arrived):
     features = norm_hbm.shape[1]
     norm = Fetch(norm_hbm, norm_held, ready.at[0])
-    weight = Weight(qkv_w, weights, arrived, 0, qkv_w.shape[1] // TILE)
-    tiles = features // TILE
-
-    def put(columns, values):
-        qkv_ref[:, columns] = values.astype(BF16)
-
-    weight.product(norm(), put)
+    weight = Weight(qkv_w, qkv_held, arrived, 0, qkv_held.shape[0])
+    weight.product(norm(), store_in(qkv_ref))
     queries = pl.ds(0, features)
     qkv_ref[:, queries] = (qkv_ref[:, queries].astype(F32) * scale).astype(BF16)
 
 
+def hold_kernel(
+    qkv_w, out_w, decode_w, qkv_hbm, mid_hbm, queries_hbm,
+    kv_kept, out_kept, decode_kept, qkv_kept, mid_kept, queries_kept,
+    ready, arrived,
+):
+    tiles = out_kept.shape[0]
+    weights = [
+        Weight(qkv_w, kv_kept, arrived, 0, 2 * tiles, tiles),
+        Weight(out_w, out_kept, arrived, 0, tiles, 0, 2 * tiles),
+        Weight(decode_w, decode_kept, arrived, 0, 2 * tiles, 0, 3 * tiles),
+    ]
+    rows = [
+        Fetch(source, kept, ready.at[i])
+        for i, (source, kept) in enumerate(((qkv_hbm, qkv_kept), (mid_hbm, mid_kept), (queries_hbm, queries_kept)))
+    ]
+    for weight in weights:
+        weight.wait()
+    for row in rows:
+        row()
+
+
 def process_kernel(
-    per_device, capacity, head_size, unroll,
-    me_ref, position_ref, first_hbm, norm_hbm, second_hbm, qkv_hbm, mid_hbm, queries_hbm, gain_hbm, labels_hbm,
-    qkv_w, out_w, decode_w,
+    per_device, capacity, head_size, unroll, decode_unroll,
+    me_ref, neighbour_ref, first_hbm, norm_hbm, second_hbm, qkv_ref, mid_ref, gain_hbm, queries_ref, labels_hbm,
+    kv_w, out_w, decode_w,
     answers_ref,
-    qkv_held, mid_held, queries_held, gain_held, labels_held, ready, picked,
-    chosen, other, attended, mesh_out, weights, arrived,
+    gain_held, labels_held, ready, picked,
+    chosen, other, attended, mesh_out,
 ):
-    features = mid_hbm.shape[1]
-    slots, devices = queries_hbm.shape[0], labels_hbm.shape[0]
-    tiles = features // TILE
+    features = mid_ref.shape[1]
     odd = me_ref[0] % 2
     for block in range(per_device):
         rows = pl.ds(block * BLOCK, BLOCK)
-        position = position_ref[block]
+        position = neighbour_ref[block] - me_ref[0] * per_device + per_device
         sides = ((first_hbm, 2 * (1 - odd)), (norm_hbm, 1), (second_hbm, 2 * odd))
         for source, side in sides:
             for place in range(per_device):
@@ -315,19 +345,12 @@
                     block_rows = source.at[pl.ds(place * BLOCK, BLOCK)]
                     pltpu.make_async_copy(block_rows, chosen.at[rows], picked.at[block]).start()
 
-    kv_weight = Weight(qkv_w, weights, arrived, 0, 2 * tiles, tiles)
-    out_weight = Weight(out_w, weights, arrived, 2 * tiles, tiles)
-    decode_weight = Weight(decode_w, weights, arrived, 3 * tiles, 2 * tiles)
-    qkv = Fetch(qkv_hbm, qkv_held, ready.at[0])
-    mid = Fetch(mid_hbm, mid_held, ready.at[1])
-    queries_rows = Fetch(queries_hbm, queries_held, ready.at[2])
-    gain = Fetch(gain_hbm, gain_held, ready.at[3])
-    labels = Fetch(labels_hbm, labels_held, ready.at[4])
+    gain = Fetch(gain_hbm, gain_held, ready.at[0])
+    labels = Fetch(labels_hbm, labels_held, ready.at[1])
     for block in range(per_device):
         rows = pl.ds(block * BLOCK, BLOCK)
         pltpu.make_async_copy(norm_hbm.at[rows], chosen.at[rows], picked.at[block]).wait()
-    kv_weight.product(chosen, store_in(other))
-    qkv_ref = qkv()
+    product(chosen, kv_w, store_in(other))
 
     @pl.loop(0, features // LANES, unroll=unroll)
     def _(pair):
@@ -345,17 +368,22 @@
             output = dot(powers.astype(BF16), values) / sums
             attended[rows, columns] = join_heads(output, head_size).astype(BF16)
 
-    mid_ref = mid()
-
     def put_out(columns, values):
         mesh_out[:, columns] = (mid_ref[:, columns].astype(F32) + values).astype(BF16)
 
-    out_weight.product(attended, put_out)
+    product(attended, out_w, put_out)
     chosen[...] = normed(mesh_out[...], gain()[...]).astype(BF16)
-    decode_weight.product(chosen, store_in(other))
-
+    product(chosen, decode_w, store_in(other))
+    decode_points(
+        per_device, capacity, head_size, decode_unroll, other, queries_ref, labels()[...], answers_ref
+    )
+
+
+def decode_points(per_device, capacity, head_size, unroll, other, queries_ref, labels, answers_ref):
+    slots, features = answers_ref.shape
+    devices = labels.shape[0]
     sender = floor_div(iota((slots, devices), 0), capacity) == iota((slots, devices), 1)
-    filled = dot_t(jnp.where(sender, 1.0, 0.0).astype(BF16), lanes_of(labels()[...], per_device, per_device))
+    filled = dot_t(jnp.where(sender, 1.0, 0.0).astype(BF16), lanes_of(labels, per_device, per_device))
     row = iota((slots, 1), 0)
     place = (row - floor_div(row, capacity) * capacity).astype(F32)
     reads, begin = [], jnp.zeros((slots, 1), F32)
@@ -364,7 +392,6 @@
         here = jnp.where((place >= begin) & (place < end), 1.0, 0.0)
         reads.append(jnp.broadcast_to(here, (slots, BLOCK)))
         begin = end
-    queries_ref = queries_rows()
 
     @pl.loop(0, features // LANES, unroll=unroll)
     def _(pair):
@@ -402,17 +429,17 @@
     weight.product(decoded, store_in(update_ref))
 
 
-def call(kernel, operands, outs, scratch, name, flops):
+def call(kernel, operands, outs, scratch, name, flops, limit=VMEM_MIB):
     return pl.pallas_call(
         kernel,
-        out_shape=[jax.ShapeDtypeStruct(shape, kind) for shape, kind in outs],
+        out_shape=[jax.ShapeDtypeStruct(*out) if isinstance(out, tuple) else out for out in outs],
         in_specs=[pl.BlockSpec(memory_space=space) for space, _ in operands],
         out_specs=[pl.BlockSpec(memory_space=VMEM) for _ in outs],
         scratch_shapes=scratch,
         name=name,
         cost_estimate=pl.CostEstimate(flops=flops, bytes_accessed=4 * MIB, transcendentals=0),
-        compiler_params=pltpu.CompilerParams(vmem_limit_bytes=VMEM_MIB * MIB),
-    )(*[value for _, value in operands])
+        compiler_params=pltpu.CompilerParams(vmem_limit_bytes=limit * MIB),
+    )(*[pltpu.with_memory_space_constraint(value, HBM) if space is HBM else value for space, value in operands])
 
 
 def held_like(*values):
@@ -455,7 +482,6 @@
     scale = head_size ** (-0.5)
     tiles = features // TILE
     me_row = me.astype(jnp.int32).reshape(1)
-    position = neighbour_block - me * per_device + per_device
     encode_row, decode_row = encode_block.reshape(1, -1), decode_block.reshape(1, -1)
     encode_grid_gain, encode_mesh_gain, process_gain, decode_grid_gain, decode_mesh_gain = [
         gain.reshape(1, -1)
@@ -522,29 +548,48 @@
         functools.partial(own_kernel, scale),
         [(HBM, process_norm), (HBM, process_qkv)],
         [((mesh_rows, 3 * features), BF16)],
-        [*held_like(process_norm), *weights_held(3 * tiles, features)],
+        [
+            *held_like(process_norm),
+            VMEM((3 * tiles, features, TILE), BF16),
+            pltpu.SemaphoreType.DMA((3 * tiles,)),
+        ],
         "own",
         flops=2_000_000_000,
     )
+    kv_w, out_w, decode_w, mesh_qkv, mesh_mid, arrived_queries = call(
+        hold_kernel,
+        [
+            (HBM, process_qkv), (HBM, process_out), (HBM, decode_keyval),
+            (HBM, mesh_qkv), (HBM, mesh_mid), (ANY, arrived_queries),
+        ],
+        [
+            *[VMEM((count * tiles, features, TILE), BF16) for count in (2, 1, 2)],
+            *[VMEM(rows.shape, BF16) for rows in (mesh_qkv, mesh_mid, arrived_queries)],
+        ],
+        [pltpu.SemaphoreType.DMA((3,)), pltpu.SemaphoreType.DMA((5 * tiles,))],
+        "hold",
+        flops=2_000_000_000,
+        limit=36,
+    )
     (answers,) = call(
-        functools.partial(process_kernel, per_device, capacity, head_size, PROCESS_UNROLL),
-        [
-            (SMEM, me_row), (SMEM, position), (ANY, first), (HBM, process_norm), (ANY, second), (HBM, mesh_qkv),
-            (HBM, mesh_mid), (ANY, arrived_queries), (HBM, decode_mesh_gain), (HBM, labels),
-            (HBM, process_qkv), (HBM, process_out), (HBM, decode_keyval),
+        functools.partial(process_kernel, per_device, capacity, head_size, PROCESS_UNROLL, DECODE_UNROLL),
+        [
+            (SMEM, me_row), (SMEM, neighbour_block), (ANY, first), (ANY, process_norm), (ANY, second),
+            (VMEM, mesh_qkv), (VMEM, mesh_mid), (HBM, decode_mesh_gain), (VMEM, arrived_queries), (HBM, labels),
+            (VMEM, kv_w), (VMEM, out_w), (VMEM, decode_w),
         ],
         [((slots, features), BF16)],
         [
-            *held_like(mesh_qkv, mesh_mid, arrived_queries, decode_mesh_gain, labels),
+            *held_like(decode_mesh_gain, labels),
             pltpu.SemaphoreType.DMA((per_device,)),
             VMEM((mesh_rows, features), BF16),
             VMEM((mesh_rows, 2 * features), BF16),
             VMEM((mesh_rows, features), BF16),
             VMEM((mesh_rows, features), BF16),
-            *weights_held(5 * tiles, features),
         ],
         "process",
-        flops=6_000_000_000,
+        flops=8_000_000_000,
+        limit=36,
     )
     replies = exchange(answers, capacity, features).reshape(slots, features)
     (update,) = call(

time: 130 us -> 118 us (0.908)
  Pallas kernels: 50.7 us -> 44.1 us
  blocking collectives: 36.4 us -> 30.6 us
  waiting for transfers between devices: 26.1 us -> 30.5 us
  starting transfers between devices: 14.9 us -> 11.9 us
    pallas_call x6 -> x7, Pallas kernels: 50.7 us -> 44.1 us  [call(): pl.pallas_call(kernel, out_shape=[jax.ShapeDtypeStruct(*out) if isinstanc...]
    all_to_all x1, blocking collectives: 36.4 us -> 30.6 us  [exchange(): lax.all_to_all(rows.reshape(devices, *shape), AXES, split_axis=0, concat_...]
    all_to_all x2, waiting for transfers between devices: 26.1 us -> 30.5 us  [exchange(): lax.all_to_all(rows.reshape(devices, *shape), AXES, split_axis=0, concat_...]
    ppermute x1, starting transfers between devices: 3.09 us -> 0.3 us  [on_device(): first = lax.ppermute(process_norm, AXES, pairs)]
  transfers between devices with their start and end apart: 4 -> 4, of which waited for: 2 -> 2; matrix products, arithmetic and copies ran while one was open for 0% -> 0% of each run, Pallas kernels for 18% -> 23%
where the time goes in v2:
time: 118 us; the launch traced here: 117 us
  Pallas kernels  44.1 us (37%)
  blocking collectives  30.6 us (26%)
  waiting for transfers between devices  30.5 us (26%)
  starting transfers between devices  11.9 us (10%)
    pallas_call x7, Pallas kernels, call(): pl.pallas_call(kernel, out_shape=[jax.ShapeDtypeStruct(*out) if isinstanc...  44.1 us
    all_to_all x1, blocking collectives, exchange(): lax.all_to_all(rows.reshape(devices, *shape), AXES, split_axis=0, concat_...  30.6 us
    all_to_all x2, waiting for transfers between devices, exchange(): lax.all_to_all(rows.reshape(devices, *shape), AXES, split_axis=0, concat_...  30.5 us
    all_to_all x2, starting transfers between devices, exchange(): lax.all_to_all(rows.reshape(devices, *shape), AXES, split_axis=0, concat_...  11 us
  transfers between devices with their start and end apart: 4, of which 2 were waited for; matrix products, arithmetic and copies ran while one was open for 0% of the time, Pallas kernels for 23%

profile of v2, /device:TPU:0, one launch (start us, length us, event | category | flops | bytes accessed | tf_op | source)
XLA Modules:
  0.0 117.4 jit_solution(17422563175268089383)
XLA Ops:
  0.0 3.2 %fill.1 = bf16[32,136,128]{2,1,0:T(8,128)(2,1)} custom-call(bf16[256,1024]{1,0:T(8,128)(2,1)} %grid_hbm.1, s32[1,256]{1,0:T(1,128)} %bitcast.21, s32[1,256]{1,0:T(1,128)} %bitcast.22, f32[1,1024]{1,0:T(1,128)} %bitcast.16), custom_call_target="tpu_custom_call" | custom-call | flops 600000000 | bytes 4194304 | tf_op jit(solution)/shard_map/fill/pallas_call | solution.py:433
  3.2 7.3 %all-to-all-start = ((bf16[32,136,128]{2,1,0:T(8,128)(2,1)}), bf16[32,136,128]{2,1,0:T(8,128)(2,1)S(1)}, u32[]{:S(2)}, u32[]{:S(2)}) async-start(bf16[32,136,128]{2,1,0:T(8,128)(2,1)} %fill.1), calls=%async_computation | async-start | bytes 2228224 | tf_op jit(solution)/shard_map/all_to_all | solution.py:492
  10.5 5.0 %queries.1 = (bf16[256,1024]{1,0:T(8,128)(2,1)}, bf16[512,1024]{1,0:T(8,128)(2,1)}) custom-call(bf16[256,1024]{1,0:T(8,128)(2,1)} %mesh_hbm.3, f32[1,1024]{1,0:T(1,128)} %bitcast.17, bf16[1024,1024]{1,0:T(8,128)(2,1)} %encode_w.1, bf16[256,1024]{1,0:T(8,128)(2,1)} %grid_hbm.1, f32[1,1024]{1,0:T(1,128)} %bitcast.18, bf16[1024,1024]{1,0:T(8,128)(2,1)} %decode_w.2, ...), custom_call_target="tpu_custom_call" | custom-call | flops 2000000000 | bytes 4194304 | tf_op jit(solution)/shard_map/queries/pallas_call | solution.py:433
  15.6 22.6 %all-to-all-done.received_hbm = bf16[32,136,128]{2,1,0:T(8,128)(2,1)S(1)} async-done(((bf16[32,136,128]{2,1,0:T(8,128)(2,1)}), bf16[32,136,128]{2,1,0:T(8,128)(2,1)S(1)}, u32[]{:S(2)}, u32[]{:S(2)}) %all-to-all-start) | async-done | bytes 1114144 | tf_op jit(solution)/shard_map/all_to_all | solution.py:492
  38.2 0.0 copy-start.2
  38.2 3.6 %all-to-all-start.1 = ((bf16[32,16,1024]{2,1,0:T(8,128)(2,1)}), bf16[32,16,1024]{2,1,0:T(8,128)(2,1)S(1)}, u32[]{:S(2)}, u32[]{:S(2)}) async-start(bf16[32,16,1024]{2,1,0:T(8,128)(2,1)} %bitcast.14), calls=%async_computation.1 | async-start | bytes 2097152 | tf_op jit(solution)/shard_map/all_to_all | solution.py:492
  41.8 0.0 copy-done.2
  41.8 12.0 %encode.1 = (bf16[256,1024]{1,0:T(8,128)(2,1)}, bf16[256,1024]{1,0:T(8,128)(2,1)}, bf16[32,128]{1,0:T(8,128)(2,1)}) custom-call(bf16[32,136,128]{2,1,0:T(8,128)(2,1)} %copy-done.2, bf16[256,1024]{1,0:T(8,128)(2,1)} %get-tuple-element.16.query_hbm, bf16[256,1024]{1,0:T(8,128)(2,1)} %mesh_hbm.3, f32[1,1024]{1,0:T(1,128)} %bitcast.19, ...), custom_call_target="tpu_custom_call" | custom-call | flops 5000000000 | bytes 4194304 | tf_op jit(solution)/shard_map/encode/pallas_call | solution.py:433
  53.8 0.3 collective-permute-start
  54.1 0.7 collective-permute-start.1
  54.8 5.3 %own.1.qkv_hbm = bf16[256,3072]{1,0:T(8,128)(2,1)} custom-call(bf16[256,1024]{1,0:T(8,128)(2,1)} %get-tuple-element.17.norm_hbm, bf16[1024,3072]{1,0:T(8,128)(2,1)} %qkv_w.3), custom_call_target="tpu_custom_call" | custom-call | flops 2000000000 | bytes 4194304 | tf_op jit(solution)/shard_map/own/pallas_call | solution.py:433
  60.1 7.9 %all-to-all-done.1 = bf16[32,16,1024]{2,1,0:T(8,128)(2,1)S(1)} async-done(((bf16[32,16,1024]{2,1,0:T(8,128)(2,1)}), bf16[32,16,1024]{2,1,0:T(8,128)(2,1)S(1)}, u32[]{:S(2)}, u32[]{:S(2)}) %all-to-all-start.1) | async-done | bytes 1048608 | tf_op jit(solution)/shard_map/all_to_all | solution.py:492
  68.0 0.0 copy-start
  68.0 0.0 copy-start.1
  68.0 4.8 %hold.1 = (bf16[4,1024,512]{2,1,0:T(8,128)(2,1)S(1)}, bf16[2,1024,512]{2,1,0:T(8,128)(2,1)S(1)}, bf16[4,1024,512]{2,1,0:T(8,128)(2,1)S(1)}, bf16[256,3072]{1,0:T...) custom-call(bf16[1024,3072]{1,0:T(8,128)(2,1)} %qkv_w.3, bf16[1024,1024]{1,0:T(8,128)(2,1)} %out_w.4, ...), custom_call_target="tpu_custom_call" | custom-call | flops 2000000000 | bytes 4194304 | tf_op jit(solution)/shard_map/hold/pallas_call | solution.py:433
  72.8 0.0 collective-permute-done.first_hbm
  72.8 0.0 collective-permute-done.1.second_hbm
  72.8 0.0 copy-done
  72.8 0.0 copy-done.1
  72.8 10.3 %process.1 = bf16[512,1024]{1,0:T(8,128)(2,1)S(1)} custom-call(s32[1]{0:T(128)} %bitcast.me_ref, s32[2]{0:T(128)S(1)} %copy-done.1, bf16[256,1024]{1,0:T(8,128)(2,1)S(1)} %collective-permute-done.first_hbm, bf16[256,1024]{1,0:T(8,128)(2,1)S(1)} %copy-done, bf16[256,1024]{1,0:T(8,128)(2,1)S(1)} %collective-permute-done.1.second_hbm, ...), custom_call_target="tpu_custom_call" | custom-call | flops 8000000000 | bytes 4194304 | tf_op jit(solution)/shard_map/process/pallas_call | solution.py:433
  83.2 30.6 %all_to_all.15 = bf16[32,16,1024]{2,1,0:T(8,128)(2,1)} all-to-all(bf16[32,16,1024]{2,1,0:T(8,128)(2,1)S(1)} %bitcast.13), channel_id=1, replica_groups=mesh['gx'=4,'gy'=8] {'gx','gy'}, dimensions={0} | all-to-all | bytes 2097152 | tf_op jit(solution)/shard_map/all_to_all | solution.py:492
  113.8 3.4 %unpack.1 = bf16[256,1024]{1,0:T(8,128)(2,1)} custom-call(bf16[512,1024]{1,0:T(8,128)(2,1)} %bitcast.15, s32[1,256]{1,0:T(1,128)} %bitcast.24, bf16[1024,1024]{1,0:T(8,128)(2,1)} %out_w.5), custom_call_target="tpu_custom_call" | custom-call | flops 1000000000 | bytes 4194304 | tf_op jit(solution)/shard_map/unpack/pallas_call | solution.py:433
Async XLA Ops:
  3.2 34.9 %all-to-all-start = ((bf16[32,136,128]{2,1,0:T(8,128)(2,1)}), bf16[32,136,128]{2,1,0:T(8,128)(2,1)S(1)}, u32[]{:S(2)}, u32[]{:S(2)}) async-start(bf16[32,136,128]{2,1,0:T(8,128)(2,1)} %fill.1), calls=%async_computation | async-start | bytes 2228224 | tf_op jit(solution)/shard_map/all_to_all | solution.py:492
  38.2 3.6 %copy-start.2 = (bf16[32,136,128]{2,1,0:T(8,128)(2,1)}, bf16[32,136,128]{2,1,0:T(8,128)(2,1)S(1)}, u32[]{:S(2)}) copy-start(bf16[32,136,128]{2,1,0:T(8,128)(2,1)S(1)} %all-to-all-done.received_hbm) | copy-start | bytes 3342340
  38.2 29.8 %all-to-all-start.1 = ((bf16[32,16,1024]{2,1,0:T(8,128)(2,1)}), bf16[32,16,1024]{2,1,0:T(8,128)(2,1)S(1)}, u32[]{:S(2)}, u32[]{:S(2)}) async-start(bf16[32,16,1024]{2,1,0:T(8,128)(2,1)} %bitcast.14), calls=%async_computation.1 | async-start | bytes 2097152 | tf_op jit(solution)/shard_map/all_to_all | solution.py:492
  53.8 19.0 %collective-permute-start = (bf16[256,1024]{1,0:T(8,128)(2,1)}, bf16[256,1024]{1,0:T(8,128)(2,1)S(1)}, u32[]{:S(2)}, u32[]{:S(2)}) collective-permute-start(bf16[256,1024]{1,0:T(8,128)(2,1)} %get-tuple-element.17.norm_hbm), channel_id=1, source_target_pairs={{0,1},{1,0},{2,3},{3,2},{4,5},{5,4},{6,7},{7,6},{8,9},{9,8},{10,11... | collective-permute-start | bytes 1572872 | tf_op jit(solution)/shard_map/ppermute | solution.py:545
  54.1 18.7 %collective-permute-start.1 = (bf16[256,1024]{1,0:T(8,128)(2,1)}, bf16[256,1024]{1,0:T(8,128)(2,1)S(1)}, u32[]{:S(2)}, u32[]{:S(2)}) collective-permute-start(bf16[256,1024]{1,0:T(8,128)(2,1)} %get-tuple-element.17.norm_hbm), channel_id=1, source_target_pairs={{1,2},{2,1},{3,4},{4,3},{5,6},{6,5},{7,8},{8,7},{9,10},{10,9},{11,... | collective-permute-start | bytes 1572872 | tf_op jit(solution)/shard_map/ppermute | solution.py:546
  68.0 4.8 %copy-start = (bf16[256,1024]{1,0:T(8,128)(2,1)S(1)}, bf16[256,1024]{1,0:T(8,128)(2,1)}, u32[]{:S(2)}) copy-start(bf16[256,1024]{1,0:T(8,128)(2,1)} %get-tuple-element.17.norm_hbm) | copy-start | bytes 1572868
  68.0 4.8 %copy-start.1 = (s32[2]{0:T(128)S(1)}, s32[2]{0:T(128)}, u32[]{:S(2)}) copy-start(s32[2]{0:T(128)} %neighbour_ref.1) | copy-start | bytes 28

commit v3 on v2

--- a/solution.py
+++ b/solution.py
@@ -110,16 +110,13 @@
             self.arrive(i)
 
     def product(self, rows, put):
-        @pl.loop(0, self.count)
-        def _(i):
-            held = self.arrive(i)
-            put(pl.ds(pl.multiple_of(i * TILE, TILE), TILE), dot(rows[...], held[...]))
+        for i in range(self.count):
+            put(pl.ds(i * TILE, TILE), dot(rows[...], self.arrive(i)[...]))
 
 
 def product(rows, held, put):
-    @pl.loop(0, held.shape[0])
-    def _(i):
-        put(pl.ds(pl.multiple_of(i * TILE, TILE), TILE), dot(rows[...], held[i]))
+    for i in range(held.shape[0]):
+        put(pl.ds(i * TILE, TILE), dot(rows[...], held[i]))
 
 
 def store_in(ref):
@@ -147,8 +144,8 @@
 
 def fill_kernel(
     devices, per_device, capacity,
-    state_hbm, encode_hbm, decode_hbm, gain_hbm, packed_ref,
-    state_held, encode_held, decode_held, gain_held, ready,
+    state_hbm, encode_hbm, decode_hbm, gain_hbm, packed_hbm,
+    state_held, encode_held, decode_held, gain_held, ready, packed_ref, sent,
 ):
     encode = Fetch(encode_hbm, encode_held, ready.at[0])
     decode = Fetch(decode_hbm, decode_held, ready.at[1])
@@ -161,22 +158,34 @@
     labels = count_lanes(block_counts(encode_hits), block_counts(decode_hits), devices, per_device)
     norm = normed(state()[...], gain()[...]).astype(BF16)
     features = norm.shape[1]
+    copies = []
+
+    def send(place):
+        copies.append(pltpu.make_async_copy(packed_ref.at[place], packed_hbm.at[place], sent.at[len(copies)]))
+        copies[-1].start()
+
     if by_tiles(capacity):
+        last = (slice(None), pl.ds(features // LANES * capacity, 8))
+        packed_ref[last] = jnp.broadcast_to(labels[:, None, :], (devices, 8, LANES))
+        send(last)
         for tile in range(features // LANES):
             columns = dot(place, norm[:, tile * LANES : (tile + 1) * LANES]).astype(BF16)
-            packed_ref[:, pl.ds(tile * capacity, capacity), :] = columns.reshape(devices, capacity, LANES)
-        last = pl.ds(features // LANES * capacity, 8)
-        packed_ref[:, last, :] = jnp.broadcast_to(labels[:, None, :], (devices, 8, LANES))
+            rows = (slice(None), pl.ds(tile * capacity, capacity))
+            packed_ref[rows] = columns.reshape(devices, capacity, LANES)
+            send(rows)
     else:
         packed_ref[:, pl.ds(0, features)] = dot(place, norm).astype(BF16)
         owner = floor_div(iota((slots, devices), 0), capacity) == iota((slots, devices), 1)
         packed_ref[:, pl.ds(features, LANES)] = dot(jnp.where(owner, 1.0, 0.0).astype(BF16), labels).astype(BF16)
+        send((slice(None), slice(None)))
+    for copy in copies:
+        copy.wait()
 
 
 def query_kernel(
     devices, per_device, capacity, scale,
     mesh_hbm, mesh_gain_hbm, encode_w, grid_hbm, grid_gain_hbm, decode_w, decode_hbm,
-    query_ref, packed_ref,
+    query_ref, packed_ref, back_ref,
     mesh_held, mesh_gain_held, grid_held, grid_gain_held, decode_held, ready,
     norm_ref, weights, arrived,
 ):
@@ -191,6 +200,7 @@
     slots = packed_ref.shape[0]
     hits = block_hits(decode()[...], devices * per_device)
     place = placement(slots_of(hits, per_device, capacity), slots)
+    back_ref[...] = place.T
     norm_ref[...] = normed(grid()[...], grid_gain()[...]).astype(BF16)
 
     def put_packed(columns, values):
@@ -416,25 +426,25 @@
         answers_ref[:, columns] = jnp.where(even, outputs[0], outputs[1]).astype(BF16)
 
 
-def unpack_kernel(
-    devices, per_device, capacity, replies_hbm, decode_hbm, out_w, update_ref,
-    decode_held, replies_held, ready, decoded, weights, arrived,
-):
-    decode = Fetch(decode_hbm, decode_held, ready.at[0])
-    replies = Fetch(replies_hbm, replies_held, ready.at[1])
-    weight = Weight(out_w, weights, arrived, 0, out_w.shape[1] // TILE)
-    hits = block_hits(decode()[...], devices * per_device)
-    place = placement(slots_of(hits, per_device, capacity), replies_hbm.shape[0])
-    decoded[...] = dot_tl(place, replies()[...]).astype(BF16)
-    weight.product(decoded, store_in(update_ref))
-
-
-def call(kernel, operands, outs, scratch, name, flops, limit=VMEM_MIB):
+def unpack_kernel(replies_ref, back_ref, out_w, update_hbm, decoded, update_ref, sent):
+    features = out_w.shape[1]
+    decoded[...] = dot(back_ref[...], replies_ref[...]).astype(BF16)
+    copies = []
+    for i in range(features // TILE):
+        columns = pl.ds(i * TILE, TILE)
+        update_ref[:, columns] = dot(decoded[...], out_w[:, columns]).astype(BF16)
+        copies.append(pltpu.make_async_copy(update_ref.at[:, columns], update_hbm.at[:, columns], sent.at[i]))
+        copies[-1].start()
+    for copy in copies:
+        copy.wait()
+
+
+def call(kernel, operands, outs, scratch, name, flops, limit=VMEM_MIB, out_space=VMEM):
     return pl.pallas_call(
         kernel,
         out_shape=[jax.ShapeDtypeStruct(*out) if isinstance(out, tuple) else out for out in outs],
         in_specs=[pl.BlockSpec(memory_space=space) for space, _ in operands],
-        out_specs=[pl.BlockSpec(memory_space=VMEM) for _ in outs],
+        out_specs=[pl.BlockSpec(memory_space=out_space) for _ in outs],
         scratch_shapes=scratch,
         name=name,
         cost_estimate=pl.CostEstimate(flops=flops, bytes_accessed=4 * MIB, transcendentals=0),
@@ -501,18 +511,23 @@
         functools.partial(fill_kernel, devices, per_device, capacity),
         [(HBM, grid_state), (HBM, encode_row), (HBM, decode_row), (HBM, encode_grid_gain)],
         [(packed_shape, BF16)],
-        held_like(grid_state, encode_row, decode_row, encode_grid_gain),
+        [
+            *held_like(grid_state, encode_row, decode_row, encode_grid_gain),
+            VMEM(packed_shape, BF16),
+            pltpu.SemaphoreType.DMA((features // LANES + 1,)),
+        ],
         "fill",
         flops=600_000_000,
+        out_space=ANY,
     )
     received = exchange(packed, *payload).reshape(packed_shape)
-    query, packed_queries = call(
+    query, packed_queries, back = call(
         functools.partial(query_kernel, devices, per_device, capacity, scale),
         [
             (HBM, mesh_state), (HBM, encode_mesh_gain), (HBM, encode_query),
             (HBM, grid_state), (HBM, decode_grid_gain), (HBM, decode_query), (HBM, decode_row),
         ],
-        [((mesh_rows, features), BF16), ((slots, features), BF16)],
+        [((mesh_rows, features), BF16), ((slots, features), BF16), ((grid_count, slots), BF16)],
         [
             *held_like(mesh_state, encode_mesh_gain, grid_state, decode_grid_gain, decode_row),
             VMEM((grid_count, features), BF16),
@@ -593,12 +608,18 @@
     )
     replies = exchange(answers, capacity, features).reshape(slots, features)
     (update,) = call(
-        functools.partial(unpack_kernel, devices, per_device, capacity),
-        [(ANY, replies), (HBM, decode_row), (HBM, decode_out)],
+        unpack_kernel,
+        [(VMEM, replies), (VMEM, back), (VMEM, decode_out)],
         [((grid_count, features), BF16)],
-        [*held_like(decode_row, replies), VMEM((grid_count, features), BF16), *weights_held(tiles, features)],
+        [
+            VMEM((grid_count, features), BF16),
+            VMEM((grid_count, features), BF16),
+            pltpu.SemaphoreType.DMA((tiles,)),
+        ],
         "unpack",
         flops=1_000_000_000,
+        limit=24,
+        out_space=ANY,
     )
     return update
 

time: 118 us -> 114 us (0.966)
  Pallas kernels: 44.1 us -> 40.8 us
    pallas_call x7, Pallas kernels: 44.1 us -> 40.8 us  [call(): pl.pallas_call(kernel, out_shape=[jax.ShapeDtypeStruct(*out) if isinstanc...]
  transfers between devices with their start and end apart: 4 -> 4, of which waited for: 2 -> 2; matrix products, arithmetic and copies ran while one was open for 0% -> 0% of each run, Pallas kernels for 23% -> 24%
where the time goes in v3:
time: 114 us
  Pallas kernels  40.8 us (36%)
  blocking collectives  30.5 us (27%)
  waiting for transfers between devices  30 us (26%)
  starting transfers between devices  12 us (11%)
    pallas_call x7, Pallas kernels, call(): pl.pallas_call(kernel, out_shape=[jax.ShapeDtypeStruct(*out) if isinstanc...  40.8 us
    all_to_all x1, blocking collectives, exchange(): lax.all_to_all(rows.reshape(devices, *shape), AXES, split_axis=0, concat_...  30.5 us
    all_to_all x2, waiting for transfers between devices, exchange(): lax.all_to_all(rows.reshape(devices, *shape), AXES, split_axis=0, concat_...  30 us
    all_to_all x2, starting transfers between devices, exchange(): lax.all_to_all(rows.reshape(devices, *shape), AXES, split_axis=0, concat_...  10.9 us
  transfers between devices with their start and end apart: 4, of which 2 were waited for; matrix products, arithmetic and copies ran while one was open for 0% of the time, Pallas kernels for 24%

profile of v3, /device:TPU:0, one launch (start us, length us, event | category | flops | bytes accessed | tf_op | source)
XLA Modules:
  0.0 113.6 jit_solution(9535864479162207336)
XLA Ops:
  0.0 3.0 %fill.1 = bf16[32,136,128]{2,1,0:T(8,128)(2,1)} custom-call(bf16[256,1024]{1,0:T(8,128)(2,1)} %grid_hbm.1, s32[1,256]{1,0:T(1,128)} %bitcast.21, s32[1,256]{1,0:T(1,128)} %bitcast.22, f32[1,1024]{1,0:T(1,128)} %bitcast.16), custom_call_target="tpu_custom_call" | custom-call | flops 600000000 | bytes 4194304 | tf_op jit(solution)/shard_map/fill/pallas_call | solution.py:443
  3.1 7.3 %all-to-all-start = ((bf16[32,136,128]{2,1,0:T(8,128)(2,1)}), bf16[32,136,128]{2,1,0:T(8,128)(2,1)S(1)}, u32[]{:S(2)}, u32[]{:S(2)}) async-start(bf16[32,136,128]{2,1,0:T(8,128)(2,1)} %fill.1), calls=%async_computation | async-start | bytes 2228224 | tf_op jit(solution)/shard_map/all_to_all | solution.py:502
  10.4 5.0 %queries.1 = (bf16[256,1024]{1,0:T(8,128)(2,1)}, bf16[512,1024]{1,0:T(8,128)(2,1)}, bf16[256,512]{1,0:T(8,128)(2,1)}) custom-call(bf16[256,1024]{1,0:T(8,128)(2,1)} %mesh_hbm.3, f32[1,1024]{1,0:T(1,128)} %bitcast.17, bf16[1024,1024]{1,0:T(8,128)(2,1)} %encode_w.1, bf16[256,1024]{1,0:T(8,128)(2,1)} %grid_hbm.1, f32[1,1024]{1,0:T(1,128)} %bitcast.18, ...), custom_call_target="tpu_custom_call" | custom-call | flops 2000000000 | bytes 4194304 | tf_op jit(solution)/shard_map/queries/pallas_call | solution.py:443
  15.4 22.6 %all-to-all-done.received_hbm = bf16[32,136,128]{2,1,0:T(8,128)(2,1)S(1)} async-done(((bf16[32,136,128]{2,1,0:T(8,128)(2,1)}), bf16[32,136,128]{2,1,0:T(8,128)(2,1)S(1)}, u32[]{:S(2)}, u32[]{:S(2)}) %all-to-all-start) | async-done | bytes 1114144 | tf_op jit(solution)/shard_map/all_to_all | solution.py:502
  38.0 0.0 copy-start.4
  38.0 3.6 %all-to-all-start.1 = ((bf16[32,16,1024]{2,1,0:T(8,128)(2,1)}), bf16[32,16,1024]{2,1,0:T(8,128)(2,1)S(1)}, u32[]{:S(2)}, u32[]{:S(2)}) async-start(bf16[32,16,1024]{2,1,0:T(8,128)(2,1)} %bitcast.15), calls=%async_computation.1 | async-start | bytes 2097152 | tf_op jit(solution)/shard_map/all_to_all | solution.py:502
  41.6 0.0 copy-done.4
  41.6 12.2 %encode.1 = (bf16[256,1024]{1,0:T(8,128)(2,1)}, bf16[256,1024]{1,0:T(8,128)(2,1)}, bf16[32,128]{1,0:T(8,128)(2,1)}) custom-call(bf16[32,136,128]{2,1,0:T(8,128)(2,1)} %copy-done.4, bf16[256,1024]{1,0:T(8,128)(2,1)} %get-tuple-element.17.query_hbm, bf16[256,1024]{1,0:T(8,128)(2,1)} %mesh_hbm.3, f32[1,1024]{1,0:T(1,128)} %bitcast.19, ...), custom_call_target="tpu_custom_call" | custom-call | flops 5000000000 | bytes 4194304 | tf_op jit(solution)/shard_map/encode/pallas_call | solution.py:443
  53.8 0.3 collective-permute-start
  54.2 0.7 collective-permute-start.1
  54.9 5.5 %own.1.qkv_hbm = bf16[256,3072]{1,0:T(8,128)(2,1)} custom-call(bf16[256,1024]{1,0:T(8,128)(2,1)} %get-tuple-element.18.norm_hbm, bf16[1024,3072]{1,0:T(8,128)(2,1)} %qkv_w.3), custom_call_target="tpu_custom_call" | custom-call | flops 2000000000 | bytes 4194304 | tf_op jit(solution)/shard_map/own/pallas_call | solution.py:443
  60.4 7.4 %all-to-all-done.1 = bf16[32,16,1024]{2,1,0:T(8,128)(2,1)S(1)} async-done(((bf16[32,16,1024]{2,1,0:T(8,128)(2,1)}), bf16[32,16,1024]{2,1,0:T(8,128)(2,1)S(1)}, u32[]{:S(2)}, u32[]{:S(2)}) %all-to-all-start.1) | async-done | bytes 1048608 | tf_op jit(solution)/shard_map/all_to_all | solution.py:502
  67.8 0.0 copy-start.1
  67.8 0.0 copy-start.3
  67.8 4.8 %hold.1 = (bf16[4,1024,512]{2,1,0:T(8,128)(2,1)S(1)}, bf16[2,1024,512]{2,1,0:T(8,128)(2,1)S(1)}, bf16[4,1024,512]{2,1,0:T(8,128)(2,1)S(1)}, bf16[256,3072]{1,0:T...) custom-call(bf16[1024,3072]{1,0:T(8,128)(2,1)} %qkv_w.3, bf16[1024,1024]{1,0:T(8,128)(2,1)} %out_w.4, ...), custom_call_target="tpu_custom_call" | custom-call | flops 2000000000 | bytes 4194304 | tf_op jit(solution)/shard_map/hold/pallas_call | solution.py:443
  72.6 0.0 collective-permute-done.first_hbm
  72.6 0.0 collective-permute-done.1.second_hbm
  72.7 0.0 copy-done.1
  72.7 0.0 copy-done.3
  72.7 0.0 copy-start.2
  72.7 8.5 %process.1 = bf16[512,1024]{1,0:T(8,128)(2,1)S(1)} custom-call(s32[1]{0:T(128)} %bitcast.me_ref, s32[2]{0:T(128)S(1)} %copy-done.3, bf16[256,1024]{1,0:T(8,128)(2,1)S(1)} %collective-permute-done.first_hbm, bf16[256,1024]{1,0:T(8,128)(2,1)S(1)} %copy-done.1, bf16[256,1024]{1,0:T(8,128)(2,1)S(1)} %collective-permute-done.1.second_hbm, ...), custom_call_target="tpu_custom_call" | custom-call | flops 8000000000 | bytes 4194304 | tf_op jit(solution)/shard_map/process/pallas_call | solution.py:443
  81.2 0.0 copy-start
  81.2 30.5 %all_to_all.15 = bf16[32,16,1024]{2,1,0:T(8,128)(2,1)S(1)} all-to-all(bf16[32,16,1024]{2,1,0:T(8,128)(2,1)S(1)} %bitcast.14), channel_id=1, replica_groups=mesh['gx'=4,'gy'=8] {'gx','gy'}, dimensions={0} | all-to-all | bytes 2097152 | tf_op jit(solution)/shard_map/all_to_all | solution.py:502
  111.8 0.0 copy-done.2
  111.8 0.0 copy-done
  111.8 1.7 %unpack.1 = bf16[256,1024]{1,0:T(8,128)(2,1)} custom-call(bf16[512,1024]{1,0:T(8,128)(2,1)S(1)} %bitcast.12, bf16[256,512]{1,0:T(8,128)(2,1)S(1)} %copy-done.2, bf16[1024,1024]{1,0:T(8,128)(2,1)S(1)} %copy-done), custom_call_target="tpu_custom_call" | custom-call | flops 1000000000 | bytes 4194304 | tf_op jit(solution)/shard_map/unpack/pallas_call | solution.py:443
Async XLA Ops:
  3.1 34.9 %all-to-all-start = ((bf16[32,136,128]{2,1,0:T(8,128)(2,1)}), bf16[32,136,128]{2,1,0:T(8,128)(2,1)S(1)}, u32[]{:S(2)}, u32[]{:S(2)}) async-start(bf16[32,136,128]{2,1,0:T(8,128)(2,1)} %fill.1), calls=%async_computation | async-start | bytes 2228224 | tf_op jit(solution)/shard_map/all_to_all | solution.py:502
  38.0 3.6 %copy-start.4 = (bf16[32,136,128]{2,1,0:T(8,128)(2,1)}, bf16[32,136,128]{2,1,0:T(8,128)(2,1)S(1)}, u32[]{:S(2)}) copy-start(bf16[32,136,128]{2,1,0:T(8,128)(2,1)S(1)} %all-to-all-done.received_hbm) | copy-start | bytes 3342340
  38.0 29.8 %all-to-all-start.1 = ((bf16[32,16,1024]{2,1,0:T(8,128)(2,1)}), bf16[32,16,1024]{2,1,0:T(8,128)(2,1)S(1)}, u32[]{:S(2)}, u32[]{:S(2)}) async-start(bf16[32,16,1024]{2,1,0:T(8,128)(2,1)} %bitcast.15), calls=%async_computation.1 | async-start | bytes 2097152 | tf_op jit(solution)/shard_map/all_to_all | solution.py:502
  53.8 18.8 %collective-permute-start = (bf16[256,1024]{1,0:T(8,128)(2,1)}, bf16[256,1024]{1,0:T(8,128)(2,1)S(1)}, u32[]{:S(2)}, u32[]{:S(2)}) collective-permute-start(bf16[256,1024]{1,0:T(8,128)(2,1)} %get-tuple-element.18.norm_hbm), channel_id=1, source_target_pairs={{0,1},{1,0},{2,3},{3,2},{4,5},{5,4},{6,7},{7,6},{8,9},{9,8},{10,11... | collective-permute-start | bytes 1572872 | tf_op jit(solution)/shard_map/ppermute | solution.py:560
  54.2 18.5 %collective-permute-start.1 = (bf16[256,1024]{1,0:T(8,128)(2,1)}, bf16[256,1024]{1,0:T(8,128)(2,1)S(1)}, u32[]{:S(2)}, u32[]{:S(2)}) collective-permute-start(bf16[256,1024]{1,0:T(8,128)(2,1)} %get-tuple-element.18.norm_hbm), channel_id=1, source_target_pairs={{1,2},{2,1},{3,4},{4,3},{5,6},{6,5},{7,8},{8,7},{9,10},{10,9},{11,... | collective-permute-start | bytes 1572872 | tf_op jit(solution)/shard_map/ppermute | solution.py:561
  67.8 4.8 %copy-start.1 = (bf16[256,1024]{1,0:T(8,128)(2,1)S(1)}, bf16[256,1024]{1,0:T(8,128)(2,1)}, u32[]{:S(2)}) copy-start(bf16[256,1024]{1,0:T(8,128)(2,1)} %get-tuple-element.18.norm_hbm) | copy-start | bytes 1572868
  67.8 4.8 %copy-start.3 = (s32[2]{0:T(128)S(1)}, s32[2]{0:T(128)}, u32[]{:S(2)}) copy-start(s32[2]{0:T(128)} %neighbour_ref.1) | copy-start | bytes 28
  72.7 39.1 %copy-start.2 = (bf16[256,512]{1,0:T(8,128)(2,1)S(1)}, bf16[256,512]{1,0:T(8,128)(2,1)}, u32[]{:S(2)}) copy-start(bf16[256,512]{1,0:T(8,128)(2,1)} %get-tuple-element.28.back_ref) | copy-start | bytes 786436
  81.2 30.5 %copy-start = (bf16[1024,1024]{1,0:T(8,128)(2,1)S(1)}, bf16[1024,1024]{1,0:T(8,128)(2,1)}, u32[]{:S(2)}) copy-start(bf16[1024,1024]{1,0:T(8,128)(2,1)} %out_w.5) | copy-start | bytes 6291460

commit v4 on v3

--- a/solution.py
+++ b/solution.py
@@ -13,6 +13,7 @@
 LANES = 128
 MASKED = -1e30
 VMEM_MIB = 56
+PARTS = 4
 ENCODE_UNROLL = 4
 PROCESS_UNROLL = 8
 DECODE_UNROLL = 8
@@ -165,19 +166,21 @@
         copies[-1].start()
 
     if by_tiles(capacity):
-        last = (slice(None), pl.ds(features // LANES * capacity, 8))
-        packed_ref[last] = jnp.broadcast_to(labels[:, None, :], (devices, 8, LANES))
-        send(last)
-        for tile in range(features // LANES):
-            columns = dot(place, norm[:, tile * LANES : (tile + 1) * LANES]).astype(BF16)
-            rows = (slice(None), pl.ds(tile * capacity, capacity))
-            packed_ref[rows] = columns.reshape(devices, capacity, LANES)
-            send(rows)
+        last = pl.ds(features // LANES * capacity, 8)
+        packed_ref[:, last] = jnp.broadcast_to(labels[:, None, :], (devices, 8, LANES))
+        part = devices // PARTS
+        for i in range(PARTS):
+            owners = pl.ds(i * part, part)
+            rows = dot(place[i * part * capacity : (i + 1) * part * capacity], norm).astype(BF16)
+            for tile in range(features // LANES):
+                columns = rows[:, tile * LANES : (tile + 1) * LANES].reshape(part, capacity, LANES)
+                packed_ref[owners, pl.ds(tile * capacity, capacity)] = columns
+            send(owners)
     else:
         packed_ref[:, pl.ds(0, features)] = dot(place, norm).astype(BF16)
         owner = floor_div(iota((slots, devices), 0), capacity) == iota((slots, devices), 1)
         packed_ref[:, pl.ds(features, LANES)] = dot(jnp.where(owner, 1.0, 0.0).astype(BF16), labels).astype(BF16)
-        send((slice(None), slice(None)))
+        send(slice(None))
     for copy in copies:
         copy.wait()
 
@@ -236,6 +239,16 @@
     rows = values.shape[0] // 2
     even = even_lanes((rows, values.shape[1]), head_size)
     return jnp.where(even, values[:rows], values[rows:])
+
+
+def share_out(powers, values):
+    output = dot(powers.astype(BF16), jnp.concatenate([values, jnp.ones_like(values)], axis=1))
+    return output[:, :LANES] / output[:, LANES:]
+
+
+def keys_first(scores):
+    powers = jnp.exp(scores - jnp.max(scores, axis=0, keepdims=True))
+    return powers.astype(BF16), 1.0 / jnp.sum(powers, axis=0, keepdims=True)
 
 
 def encode_kernel(
@@ -291,8 +304,7 @@
             queries = split_heads(query_ref[block_rows, columns], head_size)
             scores = dot_t(queries, keys) + bias[block : block + 1]
             powers = jnp.exp(scores - jnp.max(scores, axis=-1, keepdims=True))
-            sums = jnp.sum(powers, axis=-1, keepdims=True)
-            output = dot(powers.astype(BF16), values) / sums
+            output = share_out(powers, values)
             attended[block_rows, columns] = join_heads(output, head_size).astype(BF16)
 
     mesh_ref = mesh()
@@ -314,9 +326,7 @@
 
 
 def hold_kernel(
-    qkv_w, out_w, decode_w, qkv_hbm, mid_hbm, queries_hbm,
-    kv_kept, out_kept, decode_kept, qkv_kept, mid_kept, queries_kept,
-    ready, arrived,
+    qkv_w, out_w, decode_w, qkv_hbm, after_hbm, kv_kept, out_kept, decode_kept, qkv_kept, ready, arrived
 ):
     tiles = out_kept.shape[0]
     weights = [
@@ -324,25 +334,21 @@
         Weight(out_w, out_kept, arrived, 0, tiles, 0, 2 * tiles),
         Weight(decode_w, decode_kept, arrived, 0, 2 * tiles, 0, 3 * tiles),
     ]
-    rows = [
-        Fetch(source, kept, ready.at[i])
-        for i, (source, kept) in enumerate(((qkv_hbm, qkv_kept), (mid_hbm, mid_kept), (queries_hbm, queries_kept)))
-    ]
+    qkv = Fetch(qkv_hbm, qkv_kept, ready.at[0])
     for weight in weights:
         weight.wait()
-    for row in rows:
-        row()
+    qkv()
 
 
 def process_kernel(
     per_device, capacity, head_size, unroll, decode_unroll,
-    me_ref, neighbour_ref, first_hbm, norm_hbm, second_hbm, qkv_ref, mid_ref, gain_hbm, queries_ref, labels_hbm,
+    me_ref, neighbour_ref, first_hbm, norm_hbm, second_hbm, qkv_ref, mid_hbm, gain_hbm, queries_ref, labels_hbm,
     kv_w, out_w, decode_w,
     answers_ref,
-    gain_held, labels_held, ready, picked,
+    mid_held, gain_held, labels_held, ready, picked,
     chosen, other, attended, mesh_out,
 ):
-    features = mid_ref.shape[1]
+    features = mid_hbm.shape[1]
     odd = me_ref[0] % 2
     for block in range(per_device):
         rows = pl.ds(block * BLOCK, BLOCK)
@@ -355,8 +361,9 @@
                     block_rows = source.at[pl.ds(place * BLOCK, BLOCK)]
                     pltpu.make_async_copy(block_rows, chosen.at[rows], picked.at[block]).start()
 
-    gain = Fetch(gain_hbm, gain_held, ready.at[0])
-    labels = Fetch(labels_hbm, labels_held, ready.at[1])
+    mid = Fetch(mid_hbm, mid_held, ready.at[0])
+    gain = Fetch(gain_hbm, gain_held, ready.at[1])
+    labels = Fetch(labels_hbm, labels_held, ready.at[2])
     for block in range(per_device):
         rows = pl.ds(block * BLOCK, BLOCK)
         pltpu.make_async_copy(norm_hbm.at[rows], chosen.at[rows], picked.at[block]).wait()
@@ -378,6 +385,8 @@
             output = dot(powers.astype(BF16), values) / sums
             attended[rows, columns] = join_heads(output, head_size).astype(BF16)
 
+    mid_ref = mid()
+
     def put_out(columns, values):
         mesh_out[:, columns] = (mid_ref[:, columns].astype(F32) + values).astype(BF16)
 
@@ -400,7 +409,7 @@
     for block in range(per_device):
         end = begin + filled[:, block : block + 1]
         here = jnp.where((place >= begin) & (place < end), 1.0, 0.0)
-        reads.append(jnp.broadcast_to(here, (slots, BLOCK)))
+        reads.append(jnp.broadcast_to(here, (slots, LANES)) > 0.5)
         begin = end
 
     @pl.loop(0, features // LANES, unroll=unroll)
@@ -409,21 +418,25 @@
         second = pl.ds(pl.multiple_of(features + pair * LANES, LANES), LANES)
         queries = queries_ref[:, columns]
         even = even_lanes((slots, LANES), head_size)
-        outputs = []
-        for head in range(LANES // head_size):
-            picked = jnp.where(even if head == 0 else ~even, queries, jnp.zeros_like(queries))
-            scores = dot_t(picked, other[:, columns])
-            chosen_scores = scores[:, :BLOCK]
-            for block in range(1, per_device):
-                here = scores[:, block * BLOCK : (block + 1) * BLOCK]
-                chosen_scores = jnp.where(reads[block] > 0.5, here, chosen_scores)
-            powers = jnp.exp(chosen_scores - jnp.max(chosen_scores, axis=-1, keepdims=True))
-            sums = jnp.sum(powers, axis=-1, keepdims=True)
-            spread = jnp.concatenate(
-                [jnp.where(reads[block] > 0.5, powers, 0.0).astype(BF16) for block in range(per_device)], axis=1
+        zero = jnp.zeros_like(queries)
+        spread = jnp.concatenate([jnp.where(here, queries, zero) for here in reads], axis=1)
+        keys, values = [
+            jnp.concatenate(
+                [split_heads(other[pl.ds(block * BLOCK, BLOCK), side], head_size) for block in range(per_device)], axis=1
             )
-            outputs.append(dot(spread, other[:, second]) / sums)
-        answers_ref[:, columns] = jnp.where(even, outputs[0], outputs[1]).astype(BF16)
+            for side in (columns, second)
+        ]
+        scores = dot_t(spread, keys)
+        powers, sums = [], []
+        for head in range(2):
+            here = scores[:, head * BLOCK : (head + 1) * BLOCK]
+            powers.append(jnp.exp(here - jnp.max(here, axis=-1, keepdims=True)))
+            sums.append(jnp.sum(powers[head], axis=-1, keepdims=True))
+        output = dot(jnp.concatenate(powers, axis=1).astype(BF16), values)
+        answer = output[:, :LANES]
+        for block in range(1, per_device):
+            answer = jnp.where(reads[block], output[:, block * LANES : (block + 1) * LANES], answer)
+        answers_ref[:, columns] = (answer / jnp.where(even, sums[0], sums[1])).astype(BF16)
 
 
 def unpack_kernel(replies_ref, back_ref, out_w, update_hbm, decoded, update_ref, sent):
@@ -514,7 +527,7 @@
         [
             *held_like(grid_state, encode_row, decode_row, encode_grid_gain),
             VMEM(packed_shape, BF16),
-            pltpu.SemaphoreType.DMA((features // LANES + 1,)),
+            pltpu.SemaphoreType.DMA((PARTS,)),
         ],
         "fill",
         flops=600_000_000,
@@ -571,17 +584,14 @@
         "own",
         flops=2_000_000_000,
     )
-    kv_w, out_w, decode_w, mesh_qkv, mesh_mid, arrived_queries = call(
+    kv_w, out_w, decode_w, mesh_qkv = call(
         hold_kernel,
-        [
-            (HBM, process_qkv), (HBM, process_out), (HBM, decode_keyval),
-            (HBM, mesh_qkv), (HBM, mesh_mid), (ANY, arrived_queries),
-        ],
+        [(HBM, process_qkv), (HBM, process_out), (HBM, decode_keyval), (HBM, mesh_qkv), (ANY, arrived_queries)],
         [
             *[VMEM((count * tiles, features, TILE), BF16) for count in (2, 1, 2)],
-            *[VMEM(rows.shape, BF16) for rows in (mesh_qkv, mesh_mid, arrived_queries)],
-        ],
-        [pltpu.SemaphoreType.DMA((3,)), pltpu.SemaphoreType.DMA((5 * tiles,))],
+            VMEM(mesh_qkv.shape, BF16),
+        ],
+        [pltpu.SemaphoreType.DMA((1,)), pltpu.SemaphoreType.DMA((5 * tiles,))],
         "hold",
         flops=2_000_000_000,
         limit=36,
@@ -590,12 +600,12 @@
         functools.partial(process_kernel, per_device, capacity, head_size, PROCESS_UNROLL, DECODE_UNROLL),
         [
             (SMEM, me_row), (SMEM, neighbour_block), (ANY, first), (ANY, process_norm), (ANY, second),
-            (VMEM, mesh_qkv), (VMEM, mesh_mid), (HBM, decode_mesh_gain), (VMEM, arrived_queries), (HBM, labels),
+            (VMEM, mesh_qkv), (HBM, mesh_mid), (HBM, decode_mesh_gain), (VMEM, arrived_queries), (HBM, labels),
             (VMEM, kv_w), (VMEM, out_w), (VMEM, decode_w),
         ],
         [((slots, features), BF16)],
         [
-            *held_like(decode_mesh_gain, labels),
+            *held_like(mesh_mid, decode_mesh_gain, labels),
             pltpu.SemaphoreType.DMA((per_device,)),
             VMEM((mesh_rows, features), BF16),
             VMEM((mesh_rows, 2 * features), BF16),

time: 114 us -> 113 us (level)
  Pallas kernels: 40.8 us -> 38.7 us
  waiting for transfers between devices: 30 us -> 31.9 us
    pallas_call x7, Pallas kernels: 40.8 us -> 38.7 us  [call(): pl.pallas_call(kernel, out_shape=[jax.ShapeDtypeStruct(*out) if isinstanc...]
    all_to_all x2, waiting for transfers between devices: 30 us -> 31.9 us  [exchange(): lax.all_to_all(rows.reshape(devices, *shape), AXES, split_axis=0, concat_...]
  transfers between devices with their start and end apart: 4 -> 4, of which waited for: 2 -> 2; matrix products, arithmetic and copies ran while one was open for 0% -> 0% of each run, Pallas kernels for 24% -> 23%
where the time goes in v4:
time: 113 us
  Pallas kernels  38.7 us (34%)
  waiting for transfers between devices  31.9 us (28%)
  blocking collectives  29.8 us (26%)
  starting transfers between devices  11.9 us (11%)
    pallas_call x7, Pallas kernels, call(): pl.pallas_call(kernel, out_shape=[jax.ShapeDtypeStruct(*out) if isinstanc...  38.7 us
    all_to_all x2, waiting for transfers between devices, exchange(): lax.all_to_all(rows.reshape(devices, *shape), AXES, split_axis=0, concat_...  31.9 us
    all_to_all x1, blocking collectives, exchange(): lax.all_to_all(rows.reshape(devices, *shape), AXES, split_axis=0, concat_...  29.8 us
    all_to_all x2, starting transfers between devices, exchange(): lax.all_to_all(rows.reshape(devices, *shape), AXES, split_axis=0, concat_...  10.9 us
  transfers between devices with their start and end apart: 4, of which 2 were waited for; matrix products, arithmetic and copies ran while one was open for 0% of the time, Pallas kernels for 23%

profile of v4, /device:TPU:0, one launch (start us, length us, event | category | flops | bytes accessed | tf_op | source)
XLA Modules:
  0.0 112.7 jit_solution(15351615335244080247)
XLA Ops:
  0.0 2.8 %fill.1 = bf16[32,136,128]{2,1,0:T(8,128)(2,1)} custom-call(bf16[256,1024]{1,0:T(8,128)(2,1)} %grid_hbm.1, s32[1,256]{1,0:T(1,128)} %bitcast.22, s32[1,256]{1,0:T(1,128)} %bitcast.23, f32[1,1024]{1,0:T(1,128)} %bitcast.17), custom_call_target="tpu_custom_call" | custom-call | flops 600000000 | bytes 4194304 | tf_op jit(solution)/shard_map/fill/pallas_call | solution.py:456
  2.8 7.3 %all-to-all-start = ((bf16[32,136,128]{2,1,0:T(8,128)(2,1)}), bf16[32,136,128]{2,1,0:T(8,128)(2,1)S(1)}, u32[]{:S(2)}, u32[]{:S(2)}) async-start(bf16[32,136,128]{2,1,0:T(8,128)(2,1)} %fill.1), calls=%async_computation | async-start | bytes 2228224 | tf_op jit(solution)/shard_map/all_to_all | solution.py:515
  10.1 5.0 %queries.1 = (bf16[256,1024]{1,0:T(8,128)(2,1)}, bf16[512,1024]{1,0:T(8,128)(2,1)}, bf16[256,512]{1,0:T(8,128)(2,1)}) custom-call(bf16[256,1024]{1,0:T(8,128)(2,1)} %mesh_hbm.3, f32[1,1024]{1,0:T(1,128)} %bitcast.18, bf16[1024,1024]{1,0:T(8,128)(2,1)} %encode_w.1, bf16[256,1024]{1,0:T(8,128)(2,1)} %grid_hbm.1, f32[1,1024]{1,0:T(1,128)} %bitcast.19, ...), custom_call_target="tpu_custom_call" | custom-call | flops 2000000000 | bytes 4194304 | tf_op jit(solution)/shard_map/queries/pallas_call | solution.py:456
  15.2 22.6 %all-to-all-done.received_hbm = bf16[32,136,128]{2,1,0:T(8,128)(2,1)S(1)} async-done(((bf16[32,136,128]{2,1,0:T(8,128)(2,1)}), bf16[32,136,128]{2,1,0:T(8,128)(2,1)S(1)}, u32[]{:S(2)}, u32[]{:S(2)}) %all-to-all-start) | async-done | bytes 1114144 | tf_op jit(solution)/shard_map/all_to_all | solution.py:515
  37.7 0.0 copy-start.4
  37.7 3.6 %all-to-all-start.1 = ((bf16[32,16,1024]{2,1,0:T(8,128)(2,1)}), bf16[32,16,1024]{2,1,0:T(8,128)(2,1)S(1)}, u32[]{:S(2)}, u32[]{:S(2)}) async-start(bf16[32,16,1024]{2,1,0:T(8,128)(2,1)} %bitcast.16), calls=%async_computation.1 | async-start | bytes 2097152 | tf_op jit(solution)/shard_map/all_to_all | solution.py:515
  41.4 0.0 copy-done.4
  41.4 10.3 %encode.1 = (bf16[256,1024]{1,0:T(8,128)(2,1)}, bf16[256,1024]{1,0:T(8,128)(2,1)}, bf16[32,128]{1,0:T(8,128)(2,1)}) custom-call(bf16[32,136,128]{2,1,0:T(8,128)(2,1)} %copy-done.4, bf16[256,1024]{1,0:T(8,128)(2,1)} %get-tuple-element.15.query_hbm, bf16[256,1024]{1,0:T(8,128)(2,1)} %mesh_hbm.3, f32[1,1024]{1,0:T(1,128)} %bitcast.20, ...), custom_call_target="tpu_custom_call" | custom-call | flops 5000000000 | bytes 4194304 | tf_op jit(solution)/shard_map/encode/pallas_call | solution.py:456
  51.7 0.3 collective-permute-start
  52.0 0.7 collective-permute-start.1
  52.7 5.5 %own.1.qkv_hbm = bf16[256,3072]{1,0:T(8,128)(2,1)} custom-call(bf16[256,1024]{1,0:T(8,128)(2,1)} %get-tuple-element.16.norm_hbm, bf16[1024,3072]{1,0:T(8,128)(2,1)} %qkv_w.3), custom_call_target="tpu_custom_call" | custom-call | flops 2000000000 | bytes 4194304 | tf_op jit(solution)/shard_map/own/pallas_call | solution.py:456
  58.2 9.4 %all-to-all-done.1 = bf16[32,16,1024]{2,1,0:T(8,128)(2,1)S(1)} async-done(((bf16[32,16,1024]{2,1,0:T(8,128)(2,1)}), bf16[32,16,1024]{2,1,0:T(8,128)(2,1)S(1)}, u32[]{:S(2)}, u32[]{:S(2)}) %all-to-all-start.1) | async-done | bytes 1048608 | tf_op jit(solution)/shard_map/all_to_all | solution.py:515
  67.6 0.0 copy-start.1
  67.6 0.0 copy-start.3
  67.6 4.7 %hold.1 = (bf16[4,1024,512]{2,1,0:T(8,128)(2,1)S(1)}, bf16[2,1024,512]{2,1,0:T(8,128)(2,1)S(1)}, bf16[4,1024,512]{2,1,0:T(8,128)(2,1)S(1)}, bf16[256,3072]{1,0:T(8,128)(2,1)S(1)}) custom-call(bf16[1024,3072]{1,0:T(8,128)(2,1)} %qkv_w.3, bf16[1024,1024]{1,0:T(8,128)(2,1)} %out_w.4, bf16[1024,2048]{1,0:T(8,128)(2,1)} %decode_w.3, ...), custom_call_target="tpu_custom_call" | custom-call | flops 2000000000 | bytes 4194304 | tf_op jit(solution)/shard_map/hold/pallas_call | solution.py:456
  72.3 0.0 collective-permute-done.first_hbm
  72.3 0.0 collective-permute-done.1.second_hbm
  72.3 0.0 copy-done.1
  72.3 0.0 copy-done.3
  72.3 0.0 copy-start.2
  72.3 8.6 %process.1 = bf16[512,1024]{1,0:T(8,128)(2,1)S(1)} custom-call(s32[1]{0:T(128)} %bitcast.me_ref, s32[2]{0:T(128)S(1)} %copy-done.3, bf16[256,1024]{1,0:T(8,128)(2,1)S(1)} %collective-permute-done.first_hbm, bf16[256,1024]{1,0:T(8,128)(2,1)S(1)} %copy-done.1, bf16[256,1024]{1,0:T(8,128)(2,1)S(1)} %collective-permute-done.1.second_hbm, ...), custom_call_target="tpu_custom_call" | custom-call | flops 8000000000 | bytes 4194304 | tf_op jit(solution)/shard_map/process/pallas_call | solution.py:456
  81.0 0.0 copy-start
  81.0 29.8 %all_to_all.15 = bf16[32,16,1024]{2,1,0:T(8,128)(2,1)S(1)} all-to-all(bf16[32,16,1024]{2,1,0:T(8,128)(2,1)S(1)} %bitcast.15), channel_id=1, replica_groups=mesh['gx'=4,'gy'=8] {'gx','gy'}, dimensions={0} | all-to-all | bytes 2097152 | tf_op jit(solution)/shard_map/all_to_all | solution.py:515
  110.8 0.0 copy-done.2
  110.8 0.0 copy-done
  110.8 1.7 %unpack.1 = bf16[256,1024]{1,0:T(8,128)(2,1)} custom-call(bf16[512,1024]{1,0:T(8,128)(2,1)S(1)} %bitcast.12, bf16[256,512]{1,0:T(8,128)(2,1)S(1)} %copy-done.2, bf16[1024,1024]{1,0:T(8,128)(2,1)S(1)} %copy-done), custom_call_target="tpu_custom_call" | custom-call | flops 1000000000 | bytes 4194304 | tf_op jit(solution)/shard_map/unpack/pallas_call | solution.py:456
Async XLA Ops:
  2.8 34.9 %all-to-all-start = ((bf16[32,136,128]{2,1,0:T(8,128)(2,1)}), bf16[32,136,128]{2,1,0:T(8,128)(2,1)S(1)}, u32[]{:S(2)}, u32[]{:S(2)}) async-start(bf16[32,136,128]{2,1,0:T(8,128)(2,1)} %fill.1), calls=%async_computation | async-start | bytes 2228224 | tf_op jit(solution)/shard_map/all_to_all | solution.py:515
  37.7 3.6 %copy-start.4 = (bf16[32,136,128]{2,1,0:T(8,128)(2,1)}, bf16[32,136,128]{2,1,0:T(8,128)(2,1)S(1)}, u32[]{:S(2)}) copy-start(bf16[32,136,128]{2,1,0:T(8,128)(2,1)S(1)} %all-to-all-done.received_hbm) | copy-start | bytes 3342340
  37.7 29.8 %all-to-all-start.1 = ((bf16[32,16,1024]{2,1,0:T(8,128)(2,1)}), bf16[32,16,1024]{2,1,0:T(8,128)(2,1)S(1)}, u32[]{:S(2)}, u32[]{:S(2)}) async-start(bf16[32,16,1024]{2,1,0:T(8,128)(2,1)} %bitcast.16), calls=%async_computation.1 | async-start | bytes 2097152 | tf_op jit(solution)/shard_map/all_to_all | solution.py:515
  51.7 20.6 %collective-permute-start = (bf16[256,1024]{1,0:T(8,128)(2,1)}, bf16[256,1024]{1,0:T(8,128)(2,1)S(1)}, u32[]{:S(2)}, u32[]{:S(2)}) collective-permute-start(bf16[256,1024]{1,0:T(8,128)(2,1)} %get-tuple-element.16.norm_hbm), channel_id=1, source_target_pairs={{0,1},{1,0},{2,3},{3,2},{4,5},{5,4},{6,7},{7,6},{8,9},{9,8},{10,11... | collective-permute-start | bytes 1572872 | tf_op jit(solution)/shard_map/ppermute | solution.py:573
  52.0 20.3 %collective-permute-start.1 = (bf16[256,1024]{1,0:T(8,128)(2,1)}, bf16[256,1024]{1,0:T(8,128)(2,1)S(1)}, u32[]{:S(2)}, u32[]{:S(2)}) collective-permute-start(bf16[256,1024]{1,0:T(8,128)(2,1)} %get-tuple-element.16.norm_hbm), channel_id=1, source_target_pairs={{1,2},{2,1},{3,4},{4,3},{5,6},{6,5},{7,8},{8,7},{9,10},{10,9},{11,... | collective-permute-start | bytes 1572872 | tf_op jit(solution)/shard_map/ppermute | solution.py:574
  67.6 4.7 %copy-start.1 = (bf16[256,1024]{1,0:T(8,128)(2,1)S(1)}, bf16[256,1024]{1,0:T(8,128)(2,1)}, u32[]{:S(2)}) copy-start(bf16[256,1024]{1,0:T(8,128)(2,1)} %get-tuple-element.16.norm_hbm) | copy-start | bytes 1572868
  67.6 4.7 %copy-start.3 = (s32[2]{0:T(128)S(1)}, s32[2]{0:T(128)}, u32[]{:S(2)}) copy-start(s32[2]{0:T(128)} %neighbour_ref.1) | copy-start | bytes 28
  72.3 38.4 %copy-start.2 = (bf16[256,512]{1,0:T(8,128)(2,1)S(1)}, bf16[256,512]{1,0:T(8,128)(2,1)}, u32[]{:S(2)}) copy-start(bf16[256,512]{1,0:T(8,128)(2,1)} %get-tuple-element.24.back_ref) | copy-start | bytes 786436
  81.0 29.8 %copy-start = (bf16[1024,1024]{1,0:T(8,128)(2,1)S(1)}, bf16[1024,1024]{1,0:T(8,128)(2,1)}, u32[]{:S(2)}) copy-start(bf16[1024,1024]{1,0:T(8,128)(2,1)} %out_w.5) | copy-start | bytes 6291460

commit v5 on v4

--- a/solution.py
+++ b/solution.py
@@ -14,7 +14,7 @@
 MASKED = -1e30
 VMEM_MIB = 56
 PARTS = 4
-ENCODE_UNROLL = 4
+ENCODE_UNROLL = 8
 PROCESS_UNROLL = 8
 DECODE_UNROLL = 8
 ANY, HBM, VMEM, SMEM = pl.ANY, pltpu.HBM, pltpu.VMEM, pltpu.SMEM

time: 113 us -> 113 us (level)
  transfers between devices with their start and end apart: 4 -> 4, of which waited for: 2 -> 2; matrix products, arithmetic and copies ran while one was open for 0% -> 0% of each run, Pallas kernels for 23% -> 22%
where the time goes in v5:
time: 113 us
  Pallas kernels  38.2 us (34%)
  waiting for transfers between devices  32.4 us (29%)
  blocking collectives  29.8 us (26%)
  starting transfers between devices  12 us (11%)
    pallas_call x7, Pallas kernels, call(): pl.pallas_call(kernel, out_shape=[jax.ShapeDtypeStruct(*out) if isinstanc...  38.2 us
    all_to_all x2, waiting for transfers between devices, exchange(): lax.all_to_all(rows.reshape(devices, *shape), AXES, split_axis=0, concat_...  32.4 us
    all_to_all x1, blocking collectives, exchange(): lax.all_to_all(rows.reshape(devices, *shape), AXES, split_axis=0, concat_...  29.8 us
    all_to_all x2, starting transfers between devices, exchange(): lax.all_to_all(rows.reshape(devices, *shape), AXES, split_axis=0, concat_...  10.9 us
  transfers between devices with their start and end apart: 4, of which 2 were waited for; matrix products, arithmetic and copies ran while one was open for 0% of the time, Pallas kernels for 22%

profile of v5, /device:TPU:0, one launch (start us, length us, event | category | flops | bytes accessed | tf_op | source)
XLA Modules:
  0.0 112.7 jit_solution(1613569105778645248)
XLA Ops:
  0.0 2.8 %fill.1 = bf16[32,136,128]{2,1,0:T(8,128)(2,1)} custom-call(bf16[256,1024]{1,0:T(8,128)(2,1)} %grid_hbm.1, s32[1,256]{1,0:T(1,128)} %bitcast.22, s32[1,256]{1,0:T(1,128)} %bitcast.23, f32[1,1024]{1,0:T(1,128)} %bitcast.17), custom_call_target="tpu_custom_call" | custom-call | flops 600000000 | bytes 4194304 | tf_op jit(solution)/shard_map/fill/pallas_call | solution.py:456
  2.8 7.3 %all-to-all-start = ((bf16[32,136,128]{2,1,0:T(8,128)(2,1)}), bf16[32,136,128]{2,1,0:T(8,128)(2,1)S(1)}, u32[]{:S(2)}, u32[]{:S(2)}) async-start(bf16[32,136,128]{2,1,0:T(8,128)(2,1)} %fill.1), calls=%async_computation | async-start | bytes 2228224 | tf_op jit(solution)/shard_map/all_to_all | solution.py:515
  10.1 5.0 %queries.1 = (bf16[256,1024]{1,0:T(8,128)(2,1)}, bf16[512,1024]{1,0:T(8,128)(2,1)}, bf16[256,512]{1,0:T(8,128)(2,1)}) custom-call(bf16[256,1024]{1,0:T(8,128)(2,1)} %mesh_hbm.3, f32[1,1024]{1,0:T(1,128)} %bitcast.18, bf16[1024,1024]{1,0:T(8,128)(2,1)} %encode_w.1, bf16[256,1024]{1,0:T(8,128)(2,1)} %grid_hbm.1, f32[1,1024]{1,0:T(1,128)} %bitcast.19, ...), custom_call_target="tpu_custom_call" | custom-call | flops 2000000000 | bytes 4194304 | tf_op jit(solution)/shard_map/queries/pallas_call | solution.py:456
  15.2 22.6 %all-to-all-done.received_hbm = bf16[32,136,128]{2,1,0:T(8,128)(2,1)S(1)} async-done(((bf16[32,136,128]{2,1,0:T(8,128)(2,1)}), bf16[32,136,128]{2,1,0:T(8,128)(2,1)S(1)}, u32[]{:S(2)}, u32[]{:S(2)}) %all-to-all-start) | async-done | bytes 1114144 | tf_op jit(solution)/shard_map/all_to_all | solution.py:515
  37.7 0.0 copy-start.4
  37.7 3.6 %all-to-all-start.1 = ((bf16[32,16,1024]{2,1,0:T(8,128)(2,1)}), bf16[32,16,1024]{2,1,0:T(8,128)(2,1)S(1)}, u32[]{:S(2)}, u32[]{:S(2)}) async-start(bf16[32,16,1024]{2,1,0:T(8,128)(2,1)} %bitcast.16), calls=%async_computation.1 | async-start | bytes 2097152 | tf_op jit(solution)/shard_map/all_to_all | solution.py:515
  41.4 0.0 copy-done.4
  41.4 9.8 %encode.1 = (bf16[256,1024]{1,0:T(8,128)(2,1)}, bf16[256,1024]{1,0:T(8,128)(2,1)}, bf16[32,128]{1,0:T(8,128)(2,1)}) custom-call(bf16[32,136,128]{2,1,0:T(8,128)(2,1)} %copy-done.4, bf16[256,1024]{1,0:T(8,128)(2,1)} %get-tuple-element.15.query_hbm, bf16[256,1024]{1,0:T(8,128)(2,1)} %mesh_hbm.3, f32[1,1024]{1,0:T(1,128)} %bitcast.20, ...), custom_call_target="tpu_custom_call" | custom-call | flops 5000000000 | bytes 4194304 | tf_op jit(solution)/shard_map/encode/pallas_call | solution.py:456
  51.2 0.3 collective-permute-start
  51.5 0.7 collective-permute-start.1
  52.2 5.5 %own.1.qkv_hbm = bf16[256,3072]{1,0:T(8,128)(2,1)} custom-call(bf16[256,1024]{1,0:T(8,128)(2,1)} %get-tuple-element.16.norm_hbm, bf16[1024,3072]{1,0:T(8,128)(2,1)} %qkv_w.3), custom_call_target="tpu_custom_call" | custom-call | flops 2000000000 | bytes 4194304 | tf_op jit(solution)/shard_map/own/pallas_call | solution.py:456
  57.7 9.9 %all-to-all-done.1 = bf16[32,16,1024]{2,1,0:T(8,128)(2,1)S(1)} async-done(((bf16[32,16,1024]{2,1,0:T(8,128)(2,1)}), bf16[32,16,1024]{2,1,0:T(8,128)(2,1)S(1)}, u32[]{:S(2)}, u32[]{:S(2)}) %all-to-all-start.1) | async-done | bytes 1048608 | tf_op jit(solution)/shard_map/all_to_all | solution.py:515
  67.6 0.0 copy-start.1
  67.6 0.0 copy-start.3
  67.6 4.7 %hold.1 = (bf16[4,1024,512]{2,1,0:T(8,128)(2,1)S(1)}, bf16[2,1024,512]{2,1,0:T(8,128)(2,1)S(1)}, bf16[4,1024,512]{2,1,0:T(8,128)(2,1)S(1)}, bf16[256,3072]{1,0:T(8,128)(2,1)S(1)}) custom-call(bf16[1024,3072]{1,0:T(8,128)(2,1)} %qkv_w.3, bf16[1024,1024]{1,0:T(8,128)(2,1)} %out_w.4, bf16[1024,2048]{1,0:T(8,128)(2,1)} %decode_w.3, ...), custom_call_target="tpu_custom_call" | custom-call | flops 2000000000 | bytes 4194304 | tf_op jit(solution)/shard_map/hold/pallas_call | solution.py:456
  72.3 0.0 collective-permute-done.first_hbm
  72.3 0.0 collective-permute-done.1.second_hbm
  72.3 0.0 copy-done.1
  72.3 0.0 copy-done.3
  72.3 0.0 copy-start.2
  72.3 8.6 %process.1 = bf16[512,1024]{1,0:T(8,128)(2,1)S(1)} custom-call(s32[1]{0:T(128)} %bitcast.me_ref, s32[2]{0:T(128)S(1)} %copy-done.3, bf16[256,1024]{1,0:T(8,128)(2,1)S(1)} %collective-permute-done.first_hbm, bf16[256,1024]{1,0:T(8,128)(2,1)S(1)} %copy-done.1, bf16[256,1024]{1,0:T(8,128)(2,1)S(1)} %collective-permute-done.1.second_hbm, ...), custom_call_target="tpu_custom_call" | custom-call | flops 8000000000 | bytes 4194304 | tf_op jit(solution)/shard_map/process/pallas_call | solution.py:456
  81.0 0.0 copy-start
  81.0 29.8 %all_to_all.15 = bf16[32,16,1024]{2,1,0:T(8,128)(2,1)S(1)} all-to-all(bf16[32,16,1024]{2,1,0:T(8,128)(2,1)S(1)} %bitcast.15), channel_id=1, replica_groups=mesh['gx'=4,'gy'=8] {'gx','gy'}, dimensions={0} | all-to-all | bytes 2097152 | tf_op jit(solution)/shard_map/all_to_all | solution.py:515
  110.8 0.0 copy-done.2
  110.8 0.0 copy-done
  110.8 1.7 %unpack.1 = bf16[256,1024]{1,0:T(8,128)(2,1)} custom-call(bf16[512,1024]{1,0:T(8,128)(2,1)S(1)} %bitcast.12, bf16[256,512]{1,0:T(8,128)(2,1)S(1)} %copy-done.2, bf16[1024,1024]{1,0:T(8,128)(2,1)S(1)} %copy-done), custom_call_target="tpu_custom_call" | custom-call | flops 1000000000 | bytes 4194304 | tf_op jit(solution)/shard_map/unpack/pallas_call | solution.py:456
Async XLA Ops:
  2.8 34.9 %all-to-all-start = ((bf16[32,136,128]{2,1,0:T(8,128)(2,1)}), bf16[32,136,128]{2,1,0:T(8,128)(2,1)S(1)}, u32[]{:S(2)}, u32[]{:S(2)}) async-start(bf16[32,136,128]{2,1,0:T(8,128)(2,1)} %fill.1), calls=%async_computation | async-start | bytes 2228224 | tf_op jit(solution)/shard_map/all_to_all | solution.py:515
  37.7 3.6 %copy-start.4 = (bf16[32,136,128]{2,1,0:T(8,128)(2,1)}, bf16[32,136,128]{2,1,0:T(8,128)(2,1)S(1)}, u32[]{:S(2)}) copy-start(bf16[32,136,128]{2,1,0:T(8,128)(2,1)S(1)} %all-to-all-done.received_hbm) | copy-start | bytes 3342340
  37.7 29.8 %all-to-all-start.1 = ((bf16[32,16,1024]{2,1,0:T(8,128)(2,1)}), bf16[32,16,1024]{2,1,0:T(8,128)(2,1)S(1)}, u32[]{:S(2)}, u32[]{:S(2)}) async-start(bf16[32,16,1024]{2,1,0:T(8,128)(2,1)} %bitcast.16), calls=%async_computation.1 | async-start | bytes 2097152 | tf_op jit(solution)/shard_map/all_to_all | solution.py:515
  51.2 21.1 %collective-permute-start = (bf16[256,1024]{1,0:T(8,128)(2,1)}, bf16[256,1024]{1,0:T(8,128)(2,1)S(1)}, u32[]{:S(2)}, u32[]{:S(2)}) collective-permute-start(bf16[256,1024]{1,0:T(8,128)(2,1)} %get-tuple-element.16.norm_hbm), channel_id=1, source_target_pairs={{0,1},{1,0},{2,3},{3,2},{4,5},{5,4},{6,7},{7,6},{8,9},{9,8},{10,11... | collective-permute-start | bytes 1572872 | tf_op jit(solution)/shard_map/ppermute | solution.py:573
  51.5 20.8 %collective-permute-start.1 = (bf16[256,1024]{1,0:T(8,128)(2,1)}, bf16[256,1024]{1,0:T(8,128)(2,1)S(1)}, u32[]{:S(2)}, u32[]{:S(2)}) collective-permute-start(bf16[256,1024]{1,0:T(8,128)(2,1)} %get-tuple-element.16.norm_hbm), channel_id=1, source_target_pairs={{1,2},{2,1},{3,4},{4,3},{5,6},{6,5},{7,8},{8,7},{9,10},{10,9},{11,... | collective-permute-start | bytes 1572872 | tf_op jit(solution)/shard_map/ppermute | solution.py:574
  67.6 4.7 %copy-start.1 = (bf16[256,1024]{1,0:T(8,128)(2,1)S(1)}, bf16[256,1024]{1,0:T(8,128)(2,1)}, u32[]{:S(2)}) copy-start(bf16[256,1024]{1,0:T(8,128)(2,1)} %get-tuple-element.16.norm_hbm) | copy-start | bytes 1572868
  67.6 4.7 %copy-start.3 = (s32[2]{0:T(128)S(1)}, s32[2]{0:T(128)}, u32[]{:S(2)}) copy-start(s32[2]{0:T(128)} %neighbour_ref.1) | copy-start | bytes 28
  72.3 38.4 %copy-start.2 = (bf16[256,512]{1,0:T(8,128)(2,1)S(1)}, bf16[256,512]{1,0:T(8,128)(2,1)}, u32[]{:S(2)}) copy-start(bf16[256,512]{1,0:T(8,128)(2,1)} %get-tuple-element.24.back_ref) | copy-start | bytes 786436
  81.0 29.8 %copy-start = (bf16[1024,1024]{1,0:T(8,128)(2,1)S(1)}, bf16[1024,1024]{1,0:T(8,128)(2,1)}, u32[]{:S(2)}) copy-start(bf16[1024,1024]{1,0:T(8,128)(2,1)} %out_w.5) | copy-start | bytes 6291460

commit v6 on v5

--- a/solution.py
+++ b/solution.py
@@ -326,13 +326,12 @@
 
 
 def hold_kernel(
-    qkv_w, out_w, decode_w, qkv_hbm, after_hbm, kv_kept, out_kept, decode_kept, qkv_kept, ready, arrived
+    qkv_w, out_w, qkv_hbm, after_hbm, kv_kept, out_kept, qkv_kept, ready, arrived
 ):
     tiles = out_kept.shape[0]
     weights = [
         Weight(qkv_w, kv_kept, arrived, 0, 2 * tiles, tiles),
         Weight(out_w, out_kept, arrived, 0, tiles, 0, 2 * tiles),
-        Weight(decode_w, decode_kept, arrived, 0, 2 * tiles, 0, 3 * tiles),
     ]
     qkv = Fetch(qkv_hbm, qkv_kept, ready.at[0])
     for weight in weights:
@@ -346,7 +345,7 @@
     kv_w, out_w, decode_w,
     answers_ref,
     mid_held, gain_held, labels_held, ready, picked,
-    chosen, other, attended, mesh_out,
+    chosen, other, attended, mesh_out, decode_held, arrived,
 ):
     features = mid_hbm.shape[1]
     odd = me_ref[0] % 2
@@ -364,6 +363,7 @@
     mid = Fetch(mid_hbm, mid_held, ready.at[0])
     gain = Fetch(gain_hbm, gain_held, ready.at[1])
     labels = Fetch(labels_hbm, labels_held, ready.at[2])
+    decode_weight = Weight(decode_w, decode_held, arrived, 0, decode_held.shape[0])
     for block in range(per_device):
         rows = pl.ds(block * BLOCK, BLOCK)
         pltpu.make_async_copy(norm_hbm.at[rows], chosen.at[rows], picked.at[block]).wait()
@@ -392,7 +392,8 @@
 
     product(attended, out_w, put_out)
     chosen[...] = normed(mesh_out[...], gain()[...]).astype(BF16)
-    product(chosen, decode_w, store_in(other))
+    decode_weight.wait()
+    product(chosen, decode_held, store_in(other))
     decode_points(
         per_device, capacity, head_size, decode_unroll, other, queries_ref, labels()[...], answers_ref
     )
@@ -584,14 +585,14 @@
         "own",
         flops=2_000_000_000,
     )
-    kv_w, out_w, decode_w, mesh_qkv = call(
+    kv_w, out_w, mesh_qkv = call(
         hold_kernel,
-        [(HBM, process_qkv), (HBM, process_out), (HBM, decode_keyval), (HBM, mesh_qkv), (ANY, arrived_queries)],
-        [
-            *[VMEM((count * tiles, features, TILE), BF16) for count in (2, 1, 2)],
+        [(HBM, process_qkv), (HBM, process_out), (HBM, mesh_qkv), (ANY, arrived_queries)],
+        [
+            *[VMEM((count * tiles, features, TILE), BF16) for count in (2, 1)],
             VMEM(mesh_qkv.shape, BF16),
         ],
-        [pltpu.SemaphoreType.DMA((1,)), pltpu.SemaphoreType.DMA((5 * tiles,))],
+        [pltpu.SemaphoreType.DMA((1,)), pltpu.SemaphoreType.DMA((3 * tiles,))],
         "hold",
         flops=2_000_000_000,
         limit=36,
@@ -601,7 +602,7 @@
         [
             (SMEM, me_row), (SMEM, neighbour_block), (ANY, first), (ANY, process_norm), (ANY, second),
             (VMEM, mesh_qkv), (HBM, mesh_mid), (HBM, decode_mesh_gain), (VMEM, arrived_queries), (HBM, labels),
-            (VMEM, kv_w), (VMEM, out_w), (VMEM, decode_w),
+            (VMEM, kv_w), (VMEM, out_w), (HBM, decode_keyval),
         ],
         [((slots, features), BF16)],
         [
@@ -611,6 +612,7 @@
             VMEM((mesh_rows, 2 * features), BF16),
             VMEM((mesh_rows, features), BF16),
             VMEM((mesh_rows, features), BF16),
+            *weights_held(2 * tiles, features),
         ],
         "process",
         flops=8_000_000_000,

time: 113 us -> 113 us (level)
  transfers between devices with their start and end apart: 4 -> 4, of which waited for: 2 -> 2; matrix products, arithmetic and copies ran while one was open for 0% -> 0% of each run, Pallas kernels for 22% -> 21%
where the time goes in v6:
time: 113 us
  Pallas kernels  37.1 us (33%)
  waiting for transfers between devices  32.4 us (29%)
  blocking collectives  30.9 us (27%)
  starting transfers between devices  12 us (11%)
    pallas_call x7, Pallas kernels, call(): pl.pallas_call(kernel, out_shape=[jax.ShapeDtypeStruct(*out) if isinstanc...  37.1 us
    all_to_all x2, waiting for transfers between devices, exchange(): lax.all_to_all(rows.reshape(devices, *shape), AXES, split_axis=0, concat_...  32.4 us
    all_to_all x1, blocking collectives, exchange(): lax.all_to_all(rows.reshape(devices, *shape), AXES, split_axis=0, concat_...  30.9 us
    all_to_all x2, starting transfers between devices, exchange(): lax.all_to_all(rows.reshape(devices, *shape), AXES, split_axis=0, concat_...  10.9 us
  transfers between devices with their start and end apart: 4, of which 2 were waited for; matrix products, arithmetic and copies ran while one was open for 0% of the time, Pallas kernels for 21%

profile of v6, /device:TPU:0, one launch (start us, length us, event | category | flops | bytes accessed | tf_op | source)
XLA Modules:
  0.0 112.7 jit_solution(15328741202975262878)
XLA Ops:
  0.0 2.8 %fill.1 = bf16[32,136,128]{2,1,0:T(8,128)(2,1)} custom-call(bf16[256,1024]{1,0:T(8,128)(2,1)} %grid_hbm.1, s32[1,256]{1,0:T(1,128)} %bitcast.22, s32[1,256]{1,0:T(1,128)} %bitcast.23, f32[1,1024]{1,0:T(1,128)} %bitcast.17), custom_call_target="tpu_custom_call" | custom-call | flops 600000000 | bytes 4194304 | tf_op jit(solution)/shard_map/fill/pallas_call | solution.py:457
  2.8 7.3 %all-to-all-start = ((bf16[32,136,128]{2,1,0:T(8,128)(2,1)}), bf16[32,136,128]{2,1,0:T(8,128)(2,1)S(1)}, u32[]{:S(2)}, u32[]{:S(2)}) async-start(bf16[32,136,128]{2,1,0:T(8,128)(2,1)} %fill.1), calls=%async_computation | async-start | bytes 2228224 | tf_op jit(solution)/shard_map/all_to_all | solution.py:516
  10.1 5.0 %queries.1 = (bf16[256,1024]{1,0:T(8,128)(2,1)}, bf16[512,1024]{1,0:T(8,128)(2,1)}, bf16[256,512]{1,0:T(8,128)(2,1)}) custom-call(bf16[256,1024]{1,0:T(8,128)(2,1)} %mesh_hbm.3, f32[1,1024]{1,0:T(1,128)} %bitcast.18, bf16[1024,1024]{1,0:T(8,128)(2,1)} %encode_w.1, bf16[256,1024]{1,0:T(8,128)(2,1)} %grid_hbm.1, f32[1,1024]{1,0:T(1,128)} %bitcast.19, ...), custom_call_target="tpu_custom_call" | custom-call | flops 2000000000 | bytes 4194304 | tf_op jit(solution)/shard_map/queries/pallas_call | solution.py:457
  15.2 22.6 %all-to-all-done.received_hbm = bf16[32,136,128]{2,1,0:T(8,128)(2,1)S(1)} async-done(((bf16[32,136,128]{2,1,0:T(8,128)(2,1)}), bf16[32,136,128]{2,1,0:T(8,128)(2,1)S(1)}, u32[]{:S(2)}, u32[]{:S(2)}) %all-to-all-start) | async-done | bytes 1114144 | tf_op jit(solution)/shard_map/all_to_all | solution.py:516
  37.7 0.0 copy-start.4
  37.7 3.6 %all-to-all-start.1 = ((bf16[32,16,1024]{2,1,0:T(8,128)(2,1)}), bf16[32,16,1024]{2,1,0:T(8,128)(2,1)S(1)}, u32[]{:S(2)}, u32[]{:S(2)}) async-start(bf16[32,16,1024]{2,1,0:T(8,128)(2,1)} %bitcast.16), calls=%async_computation.1 | async-start | bytes 2097152 | tf_op jit(solution)/shard_map/all_to_all | solution.py:516
  41.4 0.0 copy-done.4
  41.4 9.8 %encode.1 = (bf16[256,1024]{1,0:T(8,128)(2,1)}, bf16[256,1024]{1,0:T(8,128)(2,1)}, bf16[32,128]{1,0:T(8,128)(2,1)}) custom-call(bf16[32,136,128]{2,1,0:T(8,128)(2,1)} %copy-done.4, bf16[256,1024]{1,0:T(8,128)(2,1)} %get-tuple-element.14.query_hbm, bf16[256,1024]{1,0:T(8,128)(2,1)} %mesh_hbm.3, f32[1,1024]{1,0:T(1,128)} %bitcast.20, ...), custom_call_target="tpu_custom_call" | custom-call | flops 5000000000 | bytes 4194304 | tf_op jit(solution)/shard_map/encode/pallas_call | solution.py:457
  51.2 0.3 collective-permute-start
  51.5 0.7 collective-permute-start.1
  52.2 5.5 %own.1.qkv_hbm = bf16[256,3072]{1,0:T(8,128)(2,1)} custom-call(bf16[256,1024]{1,0:T(8,128)(2,1)} %get-tuple-element.15.norm_hbm, bf16[1024,3072]{1,0:T(8,128)(2,1)} %qkv_w.3), custom_call_target="tpu_custom_call" | custom-call | flops 2000000000 | bytes 4194304 | tf_op jit(solution)/shard_map/own/pallas_call | solution.py:457
  57.7 9.9 %all-to-all-done.1 = bf16[32,16,1024]{2,1,0:T(8,128)(2,1)S(1)} async-done(((bf16[32,16,1024]{2,1,0:T(8,128)(2,1)}), bf16[32,16,1024]{2,1,0:T(8,128)(2,1)S(1)}, u32[]{:S(2)}, u32[]{:S(2)}) %all-to-all-start.1) | async-done | bytes 1048608 | tf_op jit(solution)/shard_map/all_to_all | solution.py:516
  67.6 0.0 copy-start.1
  67.6 0.0 copy-start.3
  67.6 3.4 %hold.1 = (bf16[4,1024,512]{2,1,0:T(8,128)(2,1)S(1)}, bf16[2,1024,512]{2,1,0:T(8,128)(2,1)S(1)}, bf16[256,3072]{1,0:T(8,128)(2,1)S(1)}) custom-call(bf16[1024,3072]{1,0:T(8,128)(2,1)} %qkv_w.3, bf16[1024,1024]{1,0:T(8,128)(2,1)} %out_w.4, bf16[256,3072]{1,0:T(8,128)(2,1)} %own.1.qkv_hbm, bf16[512,1024]{1,0:T(8,128)(2,1)S(1)} %bitcast.13), custom_call_target="tpu_custom_call" | custom-call | flops 2000000000 | bytes 4194304 | tf_op jit(solution)/shard_map/hold/pallas_call | solution.py:457
  71.0 0.0 collective-permute-done.first_hbm
  71.0 0.0 collective-permute-done.1.second_hbm
  71.0 0.0 copy-done.1
  71.1 0.0 copy-done.3
  71.1 0.0 copy-start.2
  71.1 8.8 %process.1 = bf16[512,1024]{1,0:T(8,128)(2,1)S(1)} custom-call(s32[1]{0:T(128)} %bitcast.me_ref, s32[2]{0:T(128)S(1)} %copy-done.3, bf16[256,1024]{1,0:T(8,128)(2,1)S(1)} %collective-permute-done.first_hbm, bf16[256,1024]{1,0:T(8,128)(2,1)S(1)} %copy-done.1, bf16[256,1024]{1,0:T(8,128)(2,1)S(1)} %collective-permute-done.1.second_hbm, ...), custom_call_target="tpu_custom_call" | custom-call | flops 8000000000 | bytes 4194304 | tf_op jit(solution)/shard_map/process/pallas_call | solution.py:457
  79.9 0.0 copy-start
  79.9 30.9 %all_to_all.15 = bf16[32,16,1024]{2,1,0:T(8,128)(2,1)S(1)} all-to-all(bf16[32,16,1024]{2,1,0:T(8,128)(2,1)S(1)} %bitcast.15), channel_id=1, replica_groups=mesh['gx'=4,'gy'=8] {'gx','gy'}, dimensions={0} | all-to-all | bytes 2097152 | tf_op jit(solution)/shard_map/all_to_all | solution.py:516
  110.8 0.0 copy-done.2
  110.8 0.0 copy-done
  110.8 1.7 %unpack.1 = bf16[256,1024]{1,0:T(8,128)(2,1)} custom-call(bf16[512,1024]{1,0:T(8,128)(2,1)S(1)} %bitcast.12, bf16[256,512]{1,0:T(8,128)(2,1)S(1)} %copy-done.2, bf16[1024,1024]{1,0:T(8,128)(2,1)S(1)} %copy-done), custom_call_target="tpu_custom_call" | custom-call | flops 1000000000 | bytes 4194304 | tf_op jit(solution)/shard_map/unpack/pallas_call | solution.py:457
Async XLA Ops:
  2.8 34.9 %all-to-all-start = ((bf16[32,136,128]{2,1,0:T(8,128)(2,1)}), bf16[32,136,128]{2,1,0:T(8,128)(2,1)S(1)}, u32[]{:S(2)}, u32[]{:S(2)}) async-start(bf16[32,136,128]{2,1,0:T(8,128)(2,1)} %fill.1), calls=%async_computation | async-start | bytes 2228224 | tf_op jit(solution)/shard_map/all_to_all | solution.py:516
  37.7 3.6 %copy-start.4 = (bf16[32,136,128]{2,1,0:T(8,128)(2,1)}, bf16[32,136,128]{2,1,0:T(8,128)(2,1)S(1)}, u32[]{:S(2)}) copy-start(bf16[32,136,128]{2,1,0:T(8,128)(2,1)S(1)} %all-to-all-done.received_hbm) | copy-start | bytes 3342340
  37.7 29.8 %all-to-all-start.1 = ((bf16[32,16,1024]{2,1,0:T(8,128)(2,1)}), bf16[32,16,1024]{2,1,0:T(8,128)(2,1)S(1)}, u32[]{:S(2)}, u32[]{:S(2)}) async-start(bf16[32,16,1024]{2,1,0:T(8,128)(2,1)} %bitcast.16), calls=%async_computation.1 | async-start | bytes 2097152 | tf_op jit(solution)/shard_map/all_to_all | solution.py:516
  51.2 19.9 %collective-permute-start = (bf16[256,1024]{1,0:T(8,128)(2,1)}, bf16[256,1024]{1,0:T(8,128)(2,1)S(1)}, u32[]{:S(2)}, u32[]{:S(2)}) collective-permute-start(bf16[256,1024]{1,0:T(8,128)(2,1)} %get-tuple-element.15.norm_hbm), channel_id=1, source_target_pairs={{0,1},{1,0},{2,3},{3,2},{4,5},{5,4},{6,7},{7,6},{8,9},{9,8},{10,11... | collective-permute-start | bytes 1572872 | tf_op jit(solution)/shard_map/ppermute | solution.py:574
  51.5 19.5 %collective-permute-start.1 = (bf16[256,1024]{1,0:T(8,128)(2,1)}, bf16[256,1024]{1,0:T(8,128)(2,1)S(1)}, u32[]{:S(2)}, u32[]{:S(2)}) collective-permute-start(bf16[256,1024]{1,0:T(8,128)(2,1)} %get-tuple-element.15.norm_hbm), channel_id=1, source_target_pairs={{1,2},{2,1},{3,4},{4,3},{5,6},{6,5},{7,8},{8,7},{9,10},{10,9},{11,... | collective-permute-start | bytes 1572872 | tf_op jit(solution)/shard_map/ppermute | solution.py:575
  67.6 3.5 %copy-start.1 = (bf16[256,1024]{1,0:T(8,128)(2,1)S(1)}, bf16[256,1024]{1,0:T(8,128)(2,1)}, u32[]{:S(2)}) copy-start(bf16[256,1024]{1,0:T(8,128)(2,1)} %get-tuple-element.15.norm_hbm) | copy-start | bytes 1572868
  67.6 3.5 %copy-start.3 = (s32[2]{0:T(128)S(1)}, s32[2]{0:T(128)}, u32[]{:S(2)}) copy-start(s32[2]{0:T(128)} %neighbour_ref.1) | copy-start | bytes 28
  71.1 39.8 %copy-start.2 = (bf16[256,512]{1,0:T(8,128)(2,1)S(1)}, bf16[256,512]{1,0:T(8,128)(2,1)}, u32[]{:S(2)}) copy-start(bf16[256,512]{1,0:T(8,128)(2,1)} %get-tuple-element.22.back_ref) | copy-start | bytes 786436
  79.9 30.9 %copy-start = (bf16[1024,1024]{1,0:T(8,128)(2,1)S(1)}, bf16[1024,1024]{1,0:T(8,128)(2,1)}, u32[]{:S(2)}) copy-start(bf16[1024,1024]{1,0:T(8,128)(2,1)} %out_w.5) | copy-start | bytes 6291460
